TPU v7x, 512 devices: a whole 4x8x8 slice. The times are simulated.
512 devices in a mesh: ens: 32 (over z, y_hi, core), lon: 16 (over x, y_lo).
Axes of the slice: x: 4, y: 8 (y_hi: 2, y_lo: 4; y = y_hi * 4 + y_lo), z: 8, core: 2. Of those that a mesh axis runs over, the one named last changes fastest.
Arguments:
- fields: bfloat16 [32, 641, 4, 2048], P('ens', None, None, 'lon'), may hold values from -6 to 6
- observed: bfloat16 [72, 4, 2048], P(None, None, 'lon'), may hold values from -6 to 6
- conv_weight: float32 [641, 49], replicated, may hold values from -0.875 to 0.875
- norm_gain: float32 [641], replicated, may hold values from 0.1 to 1.9
- up_weight: bfloat16 [1282, 641], replicated, may hold values from -0.25 to 0.25
- down_weight: bfloat16 [641, 1282], replicated, may hold values from -0.15625 to 0.15625
- head_weight: bfloat16 [72, 641], replicated, may hold values from -0.25 to 0.25
Outputs:
- field_grad: bfloat16 [32, 641, 4, 2048], P('ens', None, None, 'lon')
- score_grad: float32 [32, 72, 4, 2048], P('ens', None, None, 'lon')
- conv_grad: float32 [641, 49], replicated
- gain_grad: float32 [641], replicated
All inputs are finite; a program needn't handle non-finite values.
Results may differ from a plain program's by a relative error of at most 0.015.
Values may be sent and summed in bfloat16 or wider, within the bound.
No kernel may reach another device: no remote copies, remote signals or barrier semaphores. Data moves between devices by JAX's collectives and lax.ppermute only.
A program may use at most 64 MiB of HBM per device.

v0:
```python
import functools
import jax
import jax.numpy as jnp
from jax import lax
from jax.experimental import pallas as pl
from jax.experimental.pallas import tpu as pltpu
from jax.sharding import PartitionSpec as P

softening = 0.0625
LANES, PAD, BLOCK = 128, 8, 32
F32, BF16 = jnp.float32, jnp.bfloat16
gelu_scale = 0.7978845608028654
gelu_cubic = 0.044715


def params(mib=60):
    return pltpu.CompilerParams(vmem_limit_bytes=mib * 1024 * 1024)


def onehot(row_target, width):
    at = lax.broadcasted_iota(jnp.int32, (row_target.shape[0], width), 1)
    return (at == row_target).astype(BF16)


NN, NT, TN = (((1,), (0,)), ((), ())), (((1,), (1,)), ((), ())), (((0,), (0,)), ((), ()))


def mm(x, y, dims=NN):
    return lax.dot_general(x, y, dims, preferred_element_type=F32)


def cols(tile):
    return slice(tile * LANES, (tile + 1) * LANES)


def edges(blocks):
    return jnp.concatenate([x[-3:] for x in blocks], 0), jnp.concatenate([x[:3] for x in blocks], 0)


def pack_kernel(f_hbm, ft_ref, right_ref, left_ref, flat_ref, f_ref, sems):
    channels, nrows, lons = f_ref.shape
    tall = LANES * nrows
    loads = []
    for tile in range(ft_ref.shape[2] // LANES):
        at = pl.ds(tile * LANES, min(LANES, channels - tile * LANES))
        loads.append(pltpu.make_async_copy(f_hbm.at[at], f_ref.at[at], sems.at[tile]))
        loads[tile].start()
    eye = onehot(lax.broadcasted_iota(jnp.int32, (lons, 1), 0), lons)
    for tile in range(ft_ref.shape[2] // LANES):
        count = min(LANES, channels - tile * LANES)
        loads[tile].wait()
        z = f_ref[tile * LANES : tile * LANES + count].reshape(count * nrows, lons)
        if count < LANES:
            flat_ref[tile * tall :] = jnp.zeros((tall, lons), F32)
        flat_ref[tile * tall : tile * tall + count * nrows] = z.astype(F32)
        blocks = []
        for r in range(nrows):
            x = flat_ref[pl.ds(tile * tall + r, LANES, stride=nrows), :].astype(BF16)
            blocks.append(mm(eye, x, NT))
            ft_ref[r, :, cols(tile)] = blocks[r].astype(BF16)
        fill = jnp.zeros((16 - 3 * nrows, LANES), F32)
        last, first = edges(blocks)
        right_ref[:, cols(tile)] = jnp.concatenate([last, fill], 0).astype(BF16)
        left_ref[:, cols(tile)] = jnp.concatenate([first, fill], 0).astype(BF16)


def fill_edges(x_ref, left, right):
    tiles, nrows, tall, _ = x_ref.shape
    lons = tall - 2 * PAD
    for tile in range(tiles):
        for r in range(nrows):
            x_ref[tile, r, PAD - 3 : PAD, :] = left[3 * r : 3 * r + 3, cols(tile)]
            x_ref[tile, r, PAD + lons : PAD + lons + 3, :] = right[3 * r : 3 * r + 3, cols(tile)]


def fill_fields(x_ref, ft_ref, hl_ref, hr_ref):
    tiles, nrows, tall, _ = x_ref.shape
    for tile in range(tiles):
        for r in range(nrows):
            x_ref[tile, r, PAD : tall - PAD, :] = ft_ref[r, :, cols(tile)].astype(F32)
    fill_edges(x_ref, hl_ref[...].astype(F32), hr_ref[...].astype(F32))


def start_all(pairs_of_refs, sems, first):
    copies = [pltpu.make_async_copy(a, b, sems.at[first + i]) for i, (a, b) in enumerate(pairs_of_refs)]
    for copy in copies:
        copy.start()
    return copies


def wait_all(copies):
    for copy in copies:
        copy.wait()


def conv_block(x_ref, wt_ref, tile, start, acc, flip):
    nrows = len(acc)
    tall = acc[0].shape[0]
    acc = [v.reshape(tall // 8, 8, LANES) for v in acc]
    for b in range(7):
        at = PAD + start + (3 - b if flip else b - 3)
        xs = [x_ref[tile, r, at : at + tall, :].reshape(tall // 8, 8, LANES) for r in range(nrows)]
        for a in range(7):
            w = wt_ref[tile, pl.ds(a * 7 + b, 8, stride=0), :][None]
            for r_out in range(nrows):
                r_in = r_out + a - 3
                if 0 <= r_in < nrows:
                    to, of = (r_in, r_out) if flip else (r_out, r_in)
                    acc[to] = acc[to] + w * xs[of]
    return [v.reshape(tall, LANES) for v in acc]


def forward_kernel(
    channels, ft_hbm, hl_ref, hr_ref, wt_ref, up_hbm, down_hbm, head_hbm,
    pred_ref, xhat_hbm, inv_hbm, pre_hbm,
    x_ref, normed_ref, hidden_ref, xhat_ref, inv_ref, pre_ref, up_ref, down_ref, head_ref, ft_ref, sems,
):
    fields = start_all([(ft_hbm, ft_ref)], sems, 6)
    loads = start_all([(up_hbm, up_ref), (down_hbm, down_ref), (head_hbm, head_ref)], sems, 0)
    nrows, lons, wide = ft_ref.shape
    tiles = wide // LANES
    wait_all(fields)
    fill_fields(x_ref, ft_ref, hl_ref, hr_ref)

    def conv(tile, _):
        for start in range(0, lons, BLOCK):
            acc = conv_block(x_ref, wt_ref, tile, start, [jnp.zeros((BLOCK, LANES), F32)] * nrows, False)
            for r in range(nrows):
                xhat_ref[tile, r, start : start + BLOCK, :] = acc[r]
        return 0

    lax.fori_loop(0, tiles, conv, 0)
    for r in range(nrows):
        total = xhat_ref[0, r]
        for tile in range(1, tiles):
            total = total + xhat_ref[tile, r]
        mean = jnp.sum(total, 1, keepdims=True) * (1.0 / channels)
        total = None
        for tile in range(tiles):
            offset = xhat_ref[tile, r] - mean
            xhat_ref[tile, r] = offset
            square = offset * offset
            live = channels - tile * LANES
            if live < LANES:
                square = jnp.where(lax.broadcasted_iota(jnp.int32, square.shape, 1) < live, square, 0.0)
            total = square if total is None else total + square
        inv = lax.rsqrt(jnp.sum(total, 1, keepdims=True) * (1.0 / channels) + 1e-05)
        inv_ref[r] = inv
        for tile in range(tiles):
            xhat = xhat_ref[tile, r] * inv
            xhat_ref[tile, r] = xhat
            gain = wt_ref[tile, 49:50, :]
            normed_ref[r * lons : (r + 1) * lons, cols(tile)] = (xhat * gain).astype(BF16)
    stores = start_all([(xhat_ref, xhat_hbm), (inv_ref, inv_hbm)], sems, 3)
    wait_all(loads)
    hiddens = up_ref.shape[1]
    normed = normed_ref[:, :channels]
    for start in range(0, hiddens, 256):
        stop = min(start + 256, hiddens)
        pre = mm(normed, up_ref[:, start:stop])
        pre_ref[:, start:stop] = pre
        t = jnp.tanh(pre * (gelu_scale + (gelu_scale * gelu_cubic) * (pre * pre)))
        hidden_ref[:, start:stop] = (pre * (0.5 + 0.5 * t)).astype(BF16)
    stores += start_all([(pre_ref, pre_hbm)], sems, 5)
    lift = mm(hidden_ref[...], down_ref[...], NT)
    own = jnp.concatenate([ft_ref[r, :, :channels] for r in range(nrows)], axis=0)
    mixed = (own.astype(F32) + lift).astype(BF16)
    pred = mm(head_ref[...], mixed, NT).astype(BF16)
    pieces, deep, _ = pred_ref.shape
    per = pieces // nrows
    for p in range(pieces):
        r, i = p // per, p % per
        pred_ref[p] = pred[i * deep : (i + 1) * deep, r * lons : (r + 1) * lons]
    wait_all(stores)


def slope_kernel(pre_ref, out_ref):
    def body(i, _):
        at = pl.ds(pl.multiple_of(i * 16, 16), 16)
        pre = pre_ref[at, :]
        square = pre * pre
        t = jnp.tanh(pre * (gelu_scale + (gelu_scale * gelu_cubic) * square))
        half = 0.5 + 0.5 * t
        out_ref[at, :] = half + pre * (1.0 - t * t) * (
            0.5 * gelu_scale + (1.5 * gelu_scale * gelu_cubic) * square
        )
        return 0

    lax.fori_loop(0, pre_ref.shape[0] // 16, body, 0)


def slope(delta):
    return delta * lax.rsqrt(delta * delta + softening)


def pair_kernel(p_ref, out_ref, x_ref, twice_ref, slopes_ref):
    members, deep, lanes = p_ref.shape
    x_ref[...] = p_ref[...].astype(F32)

    def body(k, _):
        x = x_ref[:, k, :]
        twice_ref[:members] = x
        twice_ref[members:] = x
        total = jnp.zeros((members, lanes), F32)
        for d in range(1, members // 2 + 1):
            here = slope(x - twice_ref[members - d : 2 * members - d])
            total = total + here
            if 2 * d != members:
                slopes_ref[d % 2, :members] = here
                slopes_ref[d % 2, members:] = here
                total = total - slopes_ref[d % 2, d : d + members]
        out_ref[:, k, :] = total
        return 0

    lax.fori_loop(0, deep, body, 0)


def backward_kernel(
    channels, members, next_ref, pred_ref, obs_ref, pair_ref, hl_ref, hr_ref, wt_ref,
    up_hbm, down_hbm, head_hbm, xhat_hbm, inv_hbm, gs_hbm, ft_hbm,
    score_ref, cot_hbm, direct_hbm, out_ref,
    dpre_ref, cot_ref, direct_ref, sums_ref, x_ref,
    up_ref, down_ref, head_ref, xhat_ref, inv_ref, gs_ref, ft_ref, sems,
):
    first = start_all([(head_hbm, head_ref), (down_hbm, down_ref)], sems, 2)
    second = start_all([(gs_hbm, gs_ref)], sems, 4)
    third = start_all([(up_hbm, up_ref)], sems, 5)
    fourth = start_all([(xhat_hbm, xhat_ref), (inv_hbm, inv_ref), (ft_hbm, ft_ref)], sems, 6)
    tiles, nrows, lons, _ = xhat_ref.shape
    points = nrows * lons
    pieces, deep, _ = pred_ref.shape
    per = pieces // nrows
    for p in range(pieces):
        r, i = p // per, p % per
        rows, at = slice(i * deep, (i + 1) * deep), slice(r * lons, (r + 1) * lons)
        delta = pred_ref[p].astype(F32) - obs_ref[rows, at].astype(F32)
        score_ref[rows, at] = slope(delta) - pair_ref[p] * (1.0 / (members - 1))
    wait_all(first)
    mixed_cot = mm(score_ref[...].astype(BF16), head_ref[...], TN)
    rest = jnp.zeros((points, tiles * LANES - channels), F32)
    wide_cot = jnp.concatenate([mixed_cot, rest], 1).astype(BF16)
    for tile in range(tiles):
        direct_ref[tile] = wide_cot[:, cols(tile)]
    stores = start_all([(direct_ref, direct_hbm)], sems, 0)
    mixed_cot = mixed_cot.astype(BF16)
    hiddens = up_ref.shape[1]
    for start in range(0, hiddens, 256):
        stop = min(start + 256, hiddens)
        if start == 0:
            wait_all(second)
        hidden_cot = mm(mixed_cot, down_ref[:, start:stop]).astype(BF16).astype(F32)
        dpre_ref[:, start:stop] = (hidden_cot * gs_ref[:, start:stop]).astype(BF16)
    wait_all(third)
    normed_cot = mm(dpre_ref[...], up_ref[...], NT).astype(BF16).astype(F32)
    normed_cot = jnp.concatenate([normed_cot, rest], 1)
    wait_all(fourth)
    gains = [None] * tiles
    for r in range(nrows):
        here = slice(r * lons, (r + 1) * lons)
        first = second = None
        for tile in range(tiles):
            nc = normed_cot[here, cols(tile)]
            xhat = xhat_ref[tile, r]
            product = nc * xhat
            part = jnp.sum(product, 0, keepdims=True)
            gains[tile] = part if r == 0 else gains[tile] + part
            gain = wt_ref[tile, 49:50, :]
            scaled = nc * gain
            crossed = product * gain
            cot_ref[tile, r] = scaled
            first = scaled if first is None else first + scaled
            second = crossed if second is None else second + crossed
        first = jnp.sum(first, 1, keepdims=True) * (1.0 / channels)
        second = jnp.sum(second, 1, keepdims=True) * (1.0 / channels)
        for tile in range(tiles):
            cot_ref[tile, r] = inv_ref[r] * (cot_ref[tile, r] - first - xhat_ref[tile, r] * second)
    stores += start_all([(cot_ref, cot_hbm)], sems, 1)
    for tile in range(tiles):
        sums_ref[tile, 48:, :] = jnp.zeros((sums_ref.shape[1] - 48, LANES), F32)
        sums_ref[tile, 49:50, :] = gains[tile]


    fill_fields(x_ref, ft_ref, hl_ref, hr_ref)
    add_taps(x_ref, cot_ref, sums_ref)
    send(next_ref[0], cot_ref, sums_ref, out_ref)
    wait_all(stores)


def add_taps(x_ref, cot_ref, sums_ref):
    tiles, nrows, lons, _ = cot_ref.shape
    tall = 16

    def body(tile, _):
        for b in range(7):
            acc = [jnp.zeros((tall, LANES), F32)] * 7
            for start in range(0, lons, tall):
                at = PAD + start + b - 3
                xs = [x_ref[tile, r, at : at + tall, :] for r in range(nrows)]
                cs = [cot_ref[tile, r, start : start + tall, :] for r in range(nrows)]
                for a in range(7):
                    for r_out in range(nrows):
                        r_in = r_out + a - 3
                        if 0 <= r_in < nrows:
                            acc[a] = acc[a] + cs[r_out] * xs[r_in]
            for a in range(7):
                sums_ref[tile, a * 7 + b : a * 7 + b + 1, :] = jnp.sum(acc[a], 0, keepdims=True)
        return 0

    lax.fori_loop(0, tiles, body, 0)


def send(right, cot_ref, sums_ref, out_ref):
    tiles, nrows, _, _ = cot_ref.shape
    pieces, tall, _ = out_ref.shape
    deep = tall - 3 * nrows
    for tile in range(tiles):
        last, first = edges([cot_ref[tile, r] for r in range(nrows)])
        for p in range(pieces):
            edge = jnp.where(right == p, last, first)
            share = sums_ref[tile, p * deep : (p + 1) * deep, :]
            out_ref[p, :, cols(tile)] = jnp.concatenate([edge, share], 0).astype(BF16)


def adjoint_kernel(
    cot_hbm, hl_ref, hr_ref, wt_ref, direct_hbm, out_ref, x_ref, gather_ref, row_ref, direct_ref, sems
):
    tiles, nrows, lons, _ = cot_hbm.shape
    loads = start_all([(cot_hbm, x_ref.at[:, :, pl.ds(PAD, lons), :]), (direct_hbm, direct_ref)], sems, 0)
    channels = out_ref.shape[0]
    tall = LANES * nrows
    fill_edges(x_ref, hl_ref[...].astype(F32), hr_ref[...].astype(F32))
    target = lax.broadcasted_iota(jnp.int32, (tall, 1), 0)
    gather_ref[...] = onehot((target % nrows) * LANES + target // nrows, tall)
    wait_all(loads)

    def one(tile, count):
        for start in range(0, lons, BLOCK):
            acc = [direct_ref[tile, r * lons + start : r * lons + start + BLOCK, :].astype(F32) for r in range(nrows)]
            acc = conv_block(x_ref, wt_ref, tile, start, acc, True)
            for r in range(nrows):
                row_ref[start : start + BLOCK, cols(r)] = acc[r].astype(BF16)
        flat = mm(gather_ref[: count * nrows], row_ref[...], NT).astype(BF16)
        return flat.reshape(count, nrows, lons)

    def body(tile, _):
        out_ref[pl.ds(pl.multiple_of(tile * LANES, LANES), LANES)] = one(tile, LANES)
        return 0

    full = channels // LANES
    lax.fori_loop(0, full, body, 0)
    if full < tiles:
        got = one(full, 4 * (-(-(channels - full * LANES) // 4)))
        out_ref[full * LANES :] = got[: channels - full * LANES]


VM, HB = pltpu.VMEM, pltpu.HBM


def call(kernel, name, ins, outs, scratch=(), copies=0, flops=0, nbytes=0, mib=60):
    sems = [pltpu.SemaphoreType.DMA((copies,))] if copies else []
    return pl.pallas_call(
        kernel,
        name=name,
        out_shape=[jax.ShapeDtypeStruct(s, d) for s, d, _ in outs],
        in_specs=[pl.BlockSpec(memory_space=m) for m in ins],
        out_specs=[pl.BlockSpec(memory_space=m) for _, _, m in outs],
        scratch_shapes=[pltpu.VMEM(s, d) for s, d in scratch] + sems,
        compiler_params=params(mib),
        cost_estimate=pl.CostEstimate(flops=flops, bytes_accessed=nbytes, transcendentals=0) if nbytes else None,
    )


def pack(f):
    channels, nrows, lons = f.shape
    wide = -(-channels // LANES) * LANES
    edge = ((16, wide), BF16, VM)
    return call(
        pack_kernel, "pack", [HB], [((nrows, lons, wide), BF16, VM), edge, edge],
        [((nrows * wide, lons), F32), (f.shape, BF16)], wide // LANES, mib=16,
    )(f)


def padded_shape(ft):
    nrows, lons, wide = ft.shape
    return wide // LANES, nrows, lons + 2 * PAD, LANES


def forward(members, ft, hl, hr, wt, up, down, head):
    nrows, lons, wide = ft.shape
    points = nrows * lons
    channels, hiddens = down.shape
    xhat, inv, pre = ((wide // LANES, nrows, lons, LANES), F32), ((nrows, lons, 1), F32), ((points, hiddens), F32)
    return call(
        functools.partial(forward_kernel, channels), "forward", [HB] + [VM] * 3 + [HB] * 3,
        [((members, head.shape[0] * nrows // members, lons), BF16, VM), (*xhat, HB), (*inv, HB), (*pre, HB)],
        [(padded_shape(ft), F32), ((points, wide), BF16), ((points, hiddens), BF16), xhat, inv, pre,
         (up.shape, BF16), (down.shape, BF16), (head.shape, BF16), (ft.shape, BF16)], 7,
    )(ft, hl, hr, wt, up, down, head)


def gelu_slope(pre):
    points, hiddens = pre.shape
    tall = points // 8
    return pl.pallas_call(
        slope_kernel,
        name="slope",
        grid=(8,),
        out_shape=jax.ShapeDtypeStruct(pre.shape, F32),
        in_specs=[pl.BlockSpec((tall, hiddens), lambda i: (i, 0))],
        out_specs=pl.BlockSpec((tall, hiddens), lambda i: (i, 0)),
        compiler_params=params(),
        cost_estimate=pl.CostEstimate(flops=20 * pre.size, bytes_accessed=8 * pre.size, transcendentals=0),
    )(pre)


def backward(members, pieces, right, pred, obs, pair, hl, hr, wt, up, down, head, xhat, inv, gslope, ft):
    tiles, nrows, lons, _ = xhat.shape
    points, wide = nrows * lons, tiles * LANES
    channels, hiddens = down.shape
    sums = pieces * (4 if 4 * pieces >= 56 else 16)
    tall = 3 * nrows + sums // pieces
    direct = ((tiles, points, LANES), BF16)
    far = (up, down, head, xhat, inv, gslope, ft)
    return call(
        functools.partial(backward_kernel, channels, members), "backward", [pltpu.SMEM] + [VM] * 6 + [HB] * 7,
        [(obs.shape, F32, VM), (xhat.shape, F32, HB), (*direct, HB), ((pieces, tall, wide), BF16, VM)],
        [((points, hiddens), BF16), (xhat.shape, F32), direct, ((tiles, sums, LANES), F32), (padded_shape(ft), F32)]
        + [(v.shape, v.dtype) for v in far],
        9, 224 * xhat.size, 8 * xhat.size,
    )(right, pred, obs, pair, hl, hr, wt, *far)


def pairs(p):
    members, _, lanes = p.shape
    return call(
        pair_kernel, "pairs", [VM], [(p.shape, F32, VM)],
        [(p.shape, F32), ((2 * members, lanes), F32), ((2, 2 * members, lanes), F32)], mib=16,
    )(p)[0]


def adjoint(channels, cot, hl, hr, wt, direct):
    tiles, nrows, lons, _ = cot.shape
    tall = LANES * nrows
    return call(
        adjoint_kernel, "adjoint", [HB, VM, VM, VM, HB], [((channels, nrows, lons), BF16, VM)],
        [((tiles, nrows, lons + 2 * PAD, LANES), F32), ((tall, tall), BF16), ((lons, tall), BF16), (direct.shape, BF16)],
        2, 224 * cot.size, 8 * cot.size,
    )(cot, hl, hr, wt, direct)[0]


def ring(axis):
    n = lax.axis_size(axis)
    up = [(i, (i + 1) % n) for i in range(n)]
    return up, [(j, i) for i, j in up]


def swap_edges(to_right, to_left):
    up, down = ring("lon")
    return lax.ppermute(to_right, "lon", up), lax.ppermute(to_left, "lon", down)


def shards(fields, observed, conv_weight, norm_gain, up_weight, down_weight, head_weight):
    _, channels, nrows, lons = fields.shape
    nvars = observed.shape[0]
    members, pieces = lax.axis_size("ens"), lax.axis_size("lon")
    up_weight = up_weight.T
    ft, to_right, to_left = pack(fields[0])
    hl, hr = swap_edges(to_right, to_left)
    tiles = ft.shape[2] // LANES
    wt = jnp.concatenate([conv_weight.T, norm_gain[None]], 0)
    wt = jnp.pad(wt, ((0, 6), (0, tiles * LANES - channels))).reshape(56, tiles, LANES).transpose(1, 0, 2)
    pred, xhat, inv, pre = forward(members, ft, hl, hr, wt, up_weight, down_weight, head_weight)
    met = exchange(pred, "ens")
    pair = exchange(pairs(met), "ens")
    gslope = gelu_slope(pre)
    here = lax.axis_index("lon")
    before, after = (here + pieces - 1) % pieces, (here + 1) % pieces
    score, cot, direct, sent = backward(
        members, pieces, after[None], pred, observed.reshape(nvars, -1), pair, hl, hr, wt,
        up_weight, down_weight, head_weight, xhat, inv, gslope, ft,
    )
    met = exchange(sent, "lon")
    field_out, total = reduce_beside(
        jnp.sum(met[:, 3 * nrows :].astype(F32), 0).astype(BF16),
        lambda: adjoint(channels, cot, met[before], met[after], wt, direct),
    )
    return (field_out[None], score.reshape(1, nvars, nrows, lons), total[:49, :channels].T, total[49, :channels])


def exchange(x, axis):
    return lax.all_to_all(x, axis, 0, 0, tiled=True)


def reduce_beside(mine, work):
    deep, wide = mine.shape
    pieces = lax.axis_size("lon")
    parts = exchange(jnp.broadcast_to(mine, (lax.axis_size("ens"), deep, wide)), "ens")
    parts, done = lax.optimization_barrier((parts, work()))
    mine = jnp.sum(parts.astype(F32), 0)
    total = exchange(jnp.broadcast_to(mine, (pieces, deep, wide)), "lon")
    return done, total.reshape(pieces * deep, wide)


def solution(mesh):
    in_specs = (P("ens", None, None, "lon"), P(None, None, "lon"), P(), P(), P(), P(), P())
    out_specs = (P("ens", None, None, "lon"), P("ens", None, None, "lon"), P(), P())
    return jax.shard_map(shards, mesh=mesh, in_specs=in_specs, out_specs=out_specs, check_vma=False)
```

profile of v0, /device:TPU:1, one launch (start us, length us, event | category | flops | bytes accessed | tf_op | source)
XLA Modules:
  0.0 145.4 jit_solution(18033082538638311721)
XLA Ops:
  0.6 1.1 copy-done.1
  1.7 2.3 %pack.1 = (bf16[4,128,768]{2,1,0:T(8,128)(2,1)S(1)}, bf16[16,768]{1,0:T(8,128)(2,1)S(1)}, bf16[16,768]{1,0:T(8,128)(2,1)S(1)}) custom-call(bf16[641,4,128]{2,1,0:T(4,128)(2,1)S(1)} %bitcast.22), custom_call_target="tpu_custom_call" | custom-call | tf_op jit(solution)/shard_map/pack/pallas_call | solution.py:377
  4.0 0.9 copy-done
  4.9 4.0 %collective-permute-start = (bf16[16,768]{1,0:T(8,128)(2,1)S(1)}, bf16[16,768]{1,0:T(8,128)(2,1)S(1)}, u32[]{:S(2)}, u32[]{:S(2)}) collective-permute-start(bf16[16,768]{1,0:T(8,128)(2,1)S(1)} %get-tuple-element.18), channel_id=1, source_target_pairs={{0,1},{1,2},{2,3},{3,4},{4,5},{5,6},{6,7},{7,8},{8,9},{9,10},{10,1... | collective-permute-start | bytes 73736 | tf_op jit(solution)/shard_map/ppermute | solution.py:459
  8.9 6.1 %collective-permute-start.1 = (bf16[16,768]{1,0:T(8,128)(2,1)S(1)}, bf16[16,768]{1,0:T(8,128)(2,1)S(1)}, u32[]{:S(2)}, u32[]{:S(2)}) collective-permute-start(bf16[16,768]{1,0:T(8,128)(2,1)S(1)} %get-tuple-element.19), channel_id=1, source_target_pairs={{1,0},{2,1},{3,2},{4,3},{5,4},{6,5},{7,6},{8,7},{9,8},{10,9},{11,1... | collective-permute-start | bytes 73736 | tf_op jit(solution)/shard_map/ppermute | solution.py:459
  15.0 0.7 broadcast_in_dim.16
  15.7 1.6 %bitcast_bitcast_fusion.wt_ref = f32[6,56,128]{2,1,0:T(8,128)} fusion(f32[1,641]{1,0:T(1,128)S(1)} %broadcast_in_dim.16, f32[49,641]{1,0:T(8,128)} %bitcast.27), kind=kLoop, calls=%fused_computation.1 | loop fusion | flops 344064 | bytes 300232 | tf_op jit(solution)/shard_map/transpose | solution.py:471
  18.0 10.1 %forward.1 = (bf16[32,9,128]{2,1,0:T(8,128)(2,1)}, f32[6,4,128,128]{3,2,1,0:T(8,128)}, f32[4,128,1]{2,1,0:T(8,128)}, f32[512,1282]{1,0:T(8,128)}) custom-call(bf16[4,128,768]{2,1,0:T(8,128)(2,1)} %copy-done, bf16[16,768]{1,0:T(8,128)(2,1)} %copy-done.4, bf16[16,768]{1,0:T(8,128)(2,1)} %copy-done.5, f32[6,56,128]{2,1,0:T(8,128)} %bitcast_bitcast_fusion.wt_ref, ...), custom_call_target="tpu_custom_call" | custom-call | tf_op jit(solution)/shard_map/forward/pallas_call | solution.py:393
  28.1 29.2 %all_to_all.25.p_ref = bf16[32,9,128]{2,1,0:T(8,128)(2,1)S(1)} all-to-all(bf16[32,9,128]{2,1,0:T(8,128)(2,1)} %get-tuple-element.20.pred_ref), channel_id=1, replica_groups=mesh['ens'=32,'lon'=16] {'ens'}, dimensions={0} | all-to-all | bytes 147456 | tf_op jit(solution)/shard_map/all_to_all | solution.py:491
  57.3 1.7 %pairs.1 = f32[32,9,128]{2,1,0:T(8,128)} custom-call(bf16[32,9,128]{2,1,0:T(8,128)(2,1)S(1)} %all_to_all.25.p_ref), custom_call_target="tpu_custom_call" | custom-call | tf_op jit(solution)/shard_map/pairs/pallas_call | solution.py:435
  59.0 4.3 %all-to-all-start.1 = ((f32[32,9,128]{2,1,0:T(8,128)}), f32[32,9,128]{2,1,0:T(8,128)S(1)}, u32[]{:S(2)}, u32[]{:S(2)}) async-start(f32[32,9,128]{2,1,0:T(8,128)} %pairs.1), calls=%async_computation.1 | async-start | bytes 524288 | tf_op jit(solution)/shard_map/all_to_all | solution.py:491
  64.0 6.6 %slope.1.gs_hbm = f32[512,1282]{1,0:T(8,128)} custom-call(f32[512,1282]{1,0:T(8,128)} %get-tuple-element.23.pre_ref), custom_call_target="tpu_custom_call" | custom-call | flops 13127680 | bytes 5251072 | tf_op jit(solution)/shard_map/slope/pallas_call | solution.py:404
  70.6 6.3 %all-to-all-done.1.pair_ref = f32[32,9,128]{2,1,0:T(8,128)S(1)} async-done(((f32[32,9,128]{2,1,0:T(8,128)}), f32[32,9,128]{2,1,0:T(8,128)S(1)}, u32[]{:S(2)}, u32[]{:S(2)}) %all-to-all-start.1) | async-done | bytes 147488 | tf_op jit(solution)/shard_map/all_to_all | solution.py:491
  76.9 0.7 copy-done.2
  77.6 12.2 %backward.1 = (f32[72,512]{1,0:T(8,128)}, f32[6,4,128,128]{3,2,1,0:T(8,128)}, bf16[6,512,128]{2,1,0:T(8,128)(2,1)}, bf16[16,16,768]{2,1,0:T(8,128)(2,1)}) custom-call(s32[1]{0:T(128)} %bitcast.next_ref, bf16[32,9,128]{2,1,0:T(8,128)(2,1)} %get-tuple-element.20.pred_ref, bf16[72,512]{1,0:T(8,128)(2,1)} %bitcast.26, f32[32,9,128]{2,1,0:T(8,128)} %copy-done.2, ...), custom_call_target="tpu_custom_call" | custom-call | flops 88080384 | bytes 3145728 | tf_op jit(solution)/shard_map/backward/pallas_call | solution.py:424
  89.8 19.5 %all_to_all.26 = bf16[16,16,768]{2,1,0:T(8,128)(2,1)S(1)} all-to-all(bf16[16,16,768]{2,1,0:T(8,128)(2,1)} %get-tuple-element.24), channel_id=1, replica_groups=mesh['ens'=32,'lon'=16] {'lon'}, dimensions={0} | all-to-all | bytes 786432 | tf_op jit(solution)/shard_map/all_to_all | solution.py:491
  109.4 0.7 broadcast_in_dim.17
  110.1 7.1 %all-to-all-start.3 = ((bf16[32,4,768]{2,1,0:T(4,128)(2,1)}), bf16[32,4,768]{2,1,0:T(4,128)(2,1)S(1)}, u32[]{:S(2)}, u32[]{:S(2)}) async-start(bf16[32,4,768]{2,1,0:T(4,128)(2,1)} %broadcast_in_dim.17), calls=%async_computation.3 | async-start | bytes 393216 | tf_op jit(solution)/shard_map/all_to_all | solution.py:491
  117.9 8.2 %adjoint.1 = bf16[641,4,128]{2,1,0:T(4,128)(2,1)} custom-call(f32[6,4,128,128]{3,2,1,0:T(8,128)} %get-tuple-element.25.cot_hbm, bf16[16,768]{1,0:T(8,128)(2,1)} %get-tuple-element.31.hl_ref, bf16[16,768]{1,0:T(8,128)(2,1)} %get-tuple-element.30.hr_ref, f32[6,56,128]{2,1,0:T(8,128)} %bitcast_bitcast_fusion.wt_ref, ...), custom_call_target="tpu_custom_call" | custom-call | flops 88080384 | bytes 3145728 | tf_op jit(solution)/shard_map/adjoint/pallas_call | solution.py:444
  126.1 4.1 %all-to-all-done.3 = bf16[32,4,768]{2,1,0:T(4,128)(2,1)S(1)} async-done(((bf16[32,4,768]{2,1,0:T(4,128)(2,1)}), bf16[32,4,768]{2,1,0:T(4,128)(2,1)S(1)}, u32[]{:S(2)}, u32[]{:S(2)}) %all-to-all-start.3) | async-done | bytes 196640 | tf_op jit(solution)/shard_map/all_to_all | solution.py:491
  130.3 0.7 broadcast_in_dim.19
  131.0 4.3 %all-to-all-start.4 = ((f32[16,4,768]{2,1,0:T(4,128)}), f32[16,4,768]{2,1,0:T(4,128)S(1)}, u32[]{:S(2)}, u32[]{:S(2)}) async-start(f32[16,4,768]{2,1,0:T(4,128)} %broadcast_in_dim.19), calls=%async_computation.4 | async-start | bytes 393216 | tf_op jit(solution)/shard_map/all_to_all | solution.py:491
  135.4 0.7 reshape.22
  136.1 7.9 %all-to-all-done.4 = f32[16,4,768]{2,1,0:T(4,128)S(1)} async-done(((f32[16,4,768]{2,1,0:T(4,128)}), f32[16,4,768]{2,1,0:T(4,128)S(1)}, u32[]{:S(2)}, u32[]{:S(2)}) %all-to-all-start.4) | async-done | bytes 196640 | tf_op jit(solution)/shard_map/all_to_all | solution.py:491
  (20 shorter events, 3.4 us)
Async XLA Ops:
  0.6 1.1 copy-start.1
  4.0 0.9 copy-start
  4.9 12.4 %collective-permute-start = (bf16[16,768]{1,0:T(8,128)(2,1)S(1)}, bf16[16,768]{1,0:T(8,128)(2,1)S(1)}, u32[]{:S(2)}, u32[]{:S(2)}) collective-permute-start(bf16[16,768]{1,0:T(8,128)(2,1)S(1)} %get-tuple-element.18), channel_id=1, source_target_pairs={{0,1},{1,2},{2,3},{3,4},{4,5},{5,6},{6,7},{7,8},{8,9},{9,10},{10,1... | collective-permute-start | bytes 73736 | tf_op jit(solution)/shard_map/ppermute | solution.py:459
  8.9 8.4 %collective-permute-start.1 = (bf16[16,768]{1,0:T(8,128)(2,1)S(1)}, bf16[16,768]{1,0:T(8,128)(2,1)S(1)}, u32[]{:S(2)}, u32[]{:S(2)}) collective-permute-start(bf16[16,768]{1,0:T(8,128)(2,1)S(1)} %get-tuple-element.19), channel_id=1, source_target_pairs={{1,0},{2,1},{3,2},{4,3},{5,4},{6,5},{7,6},{8,7},{9,8},{10,9},{11,1... | collective-permute-start | bytes 73736 | tf_op jit(solution)/shard_map/ppermute | solution.py:459
  17.3 0.6 copy-start.4
  17.4 0.6 copy-start.5
  18.0 45.4 %copy-start.6 = (bf16[72,4,128]{2,1,0:T(4,128)(2,1)S(1)}, bf16[72,4,128]{2,1,0:T(4,128)(2,1)}, u32[]{:S(2)}) copy-start(bf16[72,4,128]{2,1,0:T(4,128)(2,1)} %param.8) | copy-start | bytes 221188
  59.0 17.9 %all-to-all-start.1 = ((f32[32,9,128]{2,1,0:T(8,128)}), f32[32,9,128]{2,1,0:T(8,128)S(1)}, u32[]{:S(2)}, u32[]{:S(2)}) async-start(f32[32,9,128]{2,1,0:T(8,128)} %pairs.1), calls=%async_computation.1 | async-start | bytes 524288 | tf_op jit(solution)/shard_map/all_to_all | solution.py:491
  76.9 0.7 copy-start.2
  110.1 20.1 %all-to-all-start.3 = ((bf16[32,4,768]{2,1,0:T(4,128)(2,1)}), bf16[32,4,768]{2,1,0:T(4,128)(2,1)S(1)}, u32[]{:S(2)}, u32[]{:S(2)}) async-start(bf16[32,4,768]{2,1,0:T(4,128)(2,1)} %broadcast_in_dim.17), calls=%async_computation.3 | async-start | bytes 393216 | tf_op jit(solution)/shard_map/all_to_all | solution.py:491
  117.9 17.5 %copy-start.3 = (f32[72,512]{1,0:T(8,128)S(1)}, f32[72,512]{1,0:T(8,128)}, u32[]{:S(2)}) copy-start(f32[72,512]{1,0:T(8,128)} %get-tuple-element.28) | copy-start | bytes 442372
  131.0 13.0 %all-to-all-start.4 = ((f32[16,4,768]{2,1,0:T(4,128)}), f32[16,4,768]{2,1,0:T(4,128)S(1)}, u32[]{:S(2)}, u32[]{:S(2)}) async-start(f32[16,4,768]{2,1,0:T(4,128)} %broadcast_in_dim.19), calls=%async_computation.4 | async-start | bytes 393216 | tf_op jit(solution)/shard_map/all_to_all | solution.py:491
where the time goes:
time: 146 us; the launch traced here: 145 us
  blocking collectives  48.7 us (33%)
  Pallas kernels  41.1 us (28%)
  starting transfers between devices  25.9 us (18%)
  waiting for transfers between devices  18.4 us (13%)
  local copies, waits for them, and re-layouts  8.74 us (6%)
  other arithmetic  1.78 us (1%)
    all_to_all x2, blocking collectives, exchange(): return lax.all_to_all(x, axis, 0, 0, tiled=True)  48.7 us
    all_to_all x3, waiting for transfers between devices, exchange(): return lax.all_to_all(x, axis, 0, 0, tiled=True)  18.4 us
    all_to_all x3, starting transfers between devices, exchange(): return lax.all_to_all(x, axis, 0, 0, tiled=True)  15.8 us
    pallas_call x1, Pallas kernels, backward(): call(functools.partial(backward_kernel, channels, members), 'backward', [...  12.2 us
    pallas_call x1, Pallas kernels, forward(): call(functools.partial(forward_kernel, channels), 'forward', [HB] + [VM]...  10.1 us
    pallas_call x1, Pallas kernels, adjoint(): call(adjoint_kernel, 'adjoint', [HB, VM, VM, VM, HB], [((channels, nrows,...  8.18 us
    pallas_call x1, Pallas kernels, gelu_slope(): pl.pallas_call(slope_kernel, name='slope', grid=(8,), out_shape=jax.Shape...  6.59 us
    ppermute x1, starting transfers between devices, swap_edges(): lax.ppermute(to_left, 'lon', down)  6.12 us
  transfers between devices with their start and end apart: 5, of which 3 were waited for; matrix products, arithmetic and copies ran while one was open for 3% of the time, Pallas kernels for 10%

commit v1 on v0

--- a/solution.py
+++ b/solution.py
@@ -37,18 +37,12 @@
     return jnp.concatenate([x[-3:] for x in blocks], 0), jnp.concatenate([x[:3] for x in blocks], 0)
 
 
-def pack_kernel(f_hbm, ft_ref, right_ref, left_ref, flat_ref, f_ref, sems):
+def pack_kernel(f_ref, ft_ref, right_ref, left_ref, flat_ref):
     channels, nrows, lons = f_ref.shape
     tall = LANES * nrows
-    loads = []
-    for tile in range(ft_ref.shape[2] // LANES):
-        at = pl.ds(tile * LANES, min(LANES, channels - tile * LANES))
-        loads.append(pltpu.make_async_copy(f_hbm.at[at], f_ref.at[at], sems.at[tile]))
-        loads[tile].start()
     eye = onehot(lax.broadcasted_iota(jnp.int32, (lons, 1), 0), lons)
     for tile in range(ft_ref.shape[2] // LANES):
         count = min(LANES, channels - tile * LANES)
-        loads[tile].wait()
         z = f_ref[tile * LANES : tile * LANES + count].reshape(count * nrows, lons)
         if count < LANES:
             flat_ref[tile * tall :] = jnp.zeros((tall, lons), F32)
@@ -181,9 +175,8 @@
         square = pre * pre
         t = jnp.tanh(pre * (gelu_scale + (gelu_scale * gelu_cubic) * square))
         half = 0.5 + 0.5 * t
-        out_ref[at, :] = half + pre * (1.0 - t * t) * (
-            0.5 * gelu_scale + (1.5 * gelu_scale * gelu_cubic) * square
-        )
+        bend = 0.5 * gelu_scale + (1.5 * gelu_scale * gelu_cubic) * square
+        out_ref[at, :] = (half + pre * (1.0 - t * t) * bend).astype(BF16)
         return 0
 
     lax.fori_loop(0, pre_ref.shape[0] // 16, body, 0)
@@ -193,7 +186,7 @@
     return delta * lax.rsqrt(delta * delta + softening)
 
 
-def pair_kernel(p_ref, out_ref, x_ref, twice_ref, slopes_ref):
+def pair_kernel(p_ref, out_ref, x_ref, twice_ref, slopes_ref, sum_ref):
     members, deep, lanes = p_ref.shape
     x_ref[...] = p_ref[...].astype(F32)
 
@@ -209,10 +202,11 @@
                 slopes_ref[d % 2, :members] = here
                 slopes_ref[d % 2, members:] = here
                 total = total - slopes_ref[d % 2, d : d + members]
-        out_ref[:, k, :] = total
+        sum_ref[:, k, :] = total
         return 0
 
     lax.fori_loop(0, deep, body, 0)
+    out_ref[...] = sum_ref[...].astype(BF16)
 
 
 def backward_kernel(
@@ -234,7 +228,7 @@
         r, i = p // per, p % per
         rows, at = slice(i * deep, (i + 1) * deep), slice(r * lons, (r + 1) * lons)
         delta = pred_ref[p].astype(F32) - obs_ref[rows, at].astype(F32)
-        score_ref[rows, at] = slope(delta) - pair_ref[p] * (1.0 / (members - 1))
+        score_ref[rows, at] = slope(delta) - pair_ref[p].astype(F32) * (1.0 / (members - 1))
     wait_all(first)
     mixed_cot = mm(score_ref[...].astype(BF16), head_ref[...], TN)
     rest = jnp.zeros((points, tiles * LANES - channels), F32)
@@ -249,7 +243,7 @@
         if start == 0:
             wait_all(second)
         hidden_cot = mm(mixed_cot, down_ref[:, start:stop]).astype(BF16).astype(F32)
-        dpre_ref[:, start:stop] = (hidden_cot * gs_ref[:, start:stop]).astype(BF16)
+        dpre_ref[:, start:stop] = (hidden_cot * gs_ref[:, start:stop].astype(F32)).astype(BF16)
     wait_all(third)
     normed_cot = mm(dpre_ref[...], up_ref[...], NT).astype(BF16).astype(F32)
     normed_cot = jnp.concatenate([normed_cot, rest], 1)
@@ -375,8 +369,8 @@
     wide = -(-channels // LANES) * LANES
     edge = ((16, wide), BF16, VM)
     return call(
-        pack_kernel, "pack", [HB], [((nrows, lons, wide), BF16, VM), edge, edge],
-        [((nrows * wide, lons), F32), (f.shape, BF16)], wide // LANES, mib=16,
+        pack_kernel, "pack", [VM], [((nrows, lons, wide), BF16, VM), edge, edge],
+        [((nrows * wide, lons), F32)], mib=16,
     )(f)
 
 
@@ -405,7 +399,7 @@
         slope_kernel,
         name="slope",
         grid=(8,),
-        out_shape=jax.ShapeDtypeStruct(pre.shape, F32),
+        out_shape=jax.ShapeDtypeStruct(pre.shape, BF16),
         in_specs=[pl.BlockSpec((tall, hiddens), lambda i: (i, 0))],
         out_specs=pl.BlockSpec((tall, hiddens), lambda i: (i, 0)),
         compiler_params=params(),
@@ -433,8 +427,8 @@
 def pairs(p):
     members, _, lanes = p.shape
     return call(
-        pair_kernel, "pairs", [VM], [(p.shape, F32, VM)],
-        [(p.shape, F32), ((2 * members, lanes), F32), ((2, 2 * members, lanes), F32)], mib=16,
+        pair_kernel, "pairs", [VM], [(p.shape, BF16, VM)],
+        [(p.shape, F32), ((2 * members, lanes), F32), ((2, 2 * members, lanes), F32), (p.shape, F32)], mib=16,
     )(p)[0]
 
 
@@ -496,8 +490,8 @@
     pieces = lax.axis_size("lon")
     parts = exchange(jnp.broadcast_to(mine, (lax.axis_size("ens"), deep, wide)), "ens")
     parts, done = lax.optimization_barrier((parts, work()))
-    mine = jnp.sum(parts.astype(F32), 0)
-    total = exchange(jnp.broadcast_to(mine, (pieces, deep, wide)), "lon")
+    mine = jnp.sum(parts.astype(F32), 0).astype(BF16)
+    total = exchange(jnp.broadcast_to(mine, (pieces, deep, wide)), "lon").astype(F32)
     return done, total.reshape(pieces * deep, wide)
 
 

time: 146 us -> 142 us (0.973)
  waiting for transfers between devices: 18.4 us -> 15.8 us
  Pallas kernels: 41.1 us -> 38.9 us
    all_to_all x3, waiting for transfers between devices: 18.4 us -> 15.8 us  [exchange(): return lax.all_to_all(x, axis, 0, 0, tiled=True)]
    pallas_call x2, Pallas kernels: 4.01 us -> 2.39 us  [the longest x1 1.71 us: pairs(): call(pair_kernel, 'pairs', [VM], [(p.shape, BF16, VM)], [(p.shape, F32),...]
where the time goes in v1:
time: 142 us
  blocking collectives  48.6 us (34%)
  Pallas kernels  38.9 us (27%)
  starting transfers between devices  27 us (19%)
  waiting for transfers between devices  15.8 us (11%)
  local copies, waits for them, and re-layouts  8.62 us (6%)
  other arithmetic  1.79 us (1%)
    all_to_all x2, blocking collectives, exchange(): return lax.all_to_all(x, axis, 0, 0, tiled=True)  48.6 us
    all_to_all x3, starting transfers between devices, exchange(): return lax.all_to_all(x, axis, 0, 0, tiled=True)  16.8 us
    all_to_all x3, waiting for transfers between devices, exchange(): return lax.all_to_all(x, axis, 0, 0, tiled=True)  15.8 us
    pallas_call x1, Pallas kernels, backward(): call(functools.partial(backward_kernel, channels, members), 'backward', [...  11.8 us
    pallas_call x1, Pallas kernels, forward(): call(functools.partial(forward_kernel, channels), 'forward', [HB] + [VM]...  10.1 us
    pallas_call x1, Pallas kernels, adjoint(): call(adjoint_kernel, 'adjoint', [HB, VM, VM, VM, HB], [((channels, nrows,...  8.18 us
    pallas_call x1, Pallas kernels, gelu_slope(): pl.pallas_call(slope_kernel, name='slope', grid=(8,), out_shape=jax.Shape...  6.4 us
    ppermute x1, starting transfers between devices, swap_edges(): lax.ppermute(to_left, 'lon', down)  6.14 us
  transfers between devices with their start and end apart: 5, of which 3 were waited for; matrix products, arithmetic and copies ran while one was open for 3% of the time, Pallas kernels for 10%

profile of v1, /device:TPU:1, one launch (start us, length us, event | category | flops | bytes accessed | tf_op | source)
XLA Modules:
  0.0 141.5 jit_solution(16014958155354679923)
XLA Ops:
  0.6 1.1 copy-done.1
  1.7 0.7 pack.1
  2.4 0.9 copy-done
  3.3 4.0 %collective-permute-start = (bf16[16,768]{1,0:T(8,128)(2,1)S(1)}, bf16[16,768]{1,0:T(8,128)(2,1)S(1)}, u32[]{:S(2)}, u32[]{:S(2)}) collective-permute-start(bf16[16,768]{1,0:T(8,128)(2,1)S(1)} %get-tuple-element.18), channel_id=1, source_target_pairs={{0,1},{1,2},{2,3},{3,4},{4,5},{5,6},{6,7},{7,8},{8,9},{9,10},{10,1... | collective-permute-start | bytes 73736 | tf_op jit(solution)/shard_map/ppermute | solution.py:453
  7.3 6.1 %collective-permute-start.1 = (bf16[16,768]{1,0:T(8,128)(2,1)S(1)}, bf16[16,768]{1,0:T(8,128)(2,1)S(1)}, u32[]{:S(2)}, u32[]{:S(2)}) collective-permute-start(bf16[16,768]{1,0:T(8,128)(2,1)S(1)} %get-tuple-element.19), channel_id=1, source_target_pairs={{1,0},{2,1},{3,2},{4,3},{5,4},{6,5},{7,6},{8,7},{9,8},{10,9},{11,1... | collective-permute-start | bytes 73736 | tf_op jit(solution)/shard_map/ppermute | solution.py:453
  13.5 0.7 broadcast_in_dim.16
  14.2 1.6 %bitcast_bitcast_fusion.wt_ref = f32[6,56,128]{2,1,0:T(8,128)} fusion(f32[1,641]{1,0:T(1,128)S(1)} %broadcast_in_dim.16, f32[49,641]{1,0:T(8,128)} %bitcast.27), kind=kLoop, calls=%fused_computation | loop fusion | flops 344064 | bytes 300232 | tf_op jit(solution)/shard_map/transpose | solution.py:465
  16.4 10.1 %forward.1 = (bf16[32,9,128]{2,1,0:T(8,128)(2,1)}, f32[6,4,128,128]{3,2,1,0:T(8,128)}, f32[4,128,1]{2,1,0:T(8,128)}, f32[512,1282]{1,0:T(8,128)}) custom-call(bf16[4,128,768]{2,1,0:T(8,128)(2,1)} %copy-done, bf16[16,768]{1,0:T(8,128)(2,1)} %copy-done.4, bf16[16,768]{1,0:T(8,128)(2,1)} %copy-done.5, f32[6,56,128]{2,1,0:T(8,128)} %bitcast_bitcast_fusion.wt_ref, ...), custom_call_target="tpu_custom_call" | custom-call | tf_op jit(solution)/shard_map/forward/pallas_call | solution.py:387
  26.5 29.2 %all_to_all.25.p_ref = bf16[32,9,128]{2,1,0:T(8,128)(2,1)S(1)} all-to-all(bf16[32,9,128]{2,1,0:T(8,128)(2,1)} %get-tuple-element.20.pred_ref), channel_id=1, replica_groups=mesh['ens'=32,'lon'=16] {'ens'}, dimensions={0} | all-to-all | bytes 147456 | tf_op jit(solution)/shard_map/all_to_all | solution.py:485
  55.7 1.7 %pairs.1 = bf16[32,9,128]{2,1,0:T(8,128)(2,1)} custom-call(bf16[32,9,128]{2,1,0:T(8,128)(2,1)S(1)} %all_to_all.25.p_ref), custom_call_target="tpu_custom_call" | custom-call | tf_op jit(solution)/shard_map/pairs/pallas_call | solution.py:429
  57.4 4.3 %all-to-all-start.1 = ((bf16[32,9,128]{2,1,0:T(8,128)(2,1)}), bf16[32,9,128]{2,1,0:T(8,128)(2,1)S(1)}, u32[]{:S(2)}, u32[]{:S(2)}) async-start(bf16[32,9,128]{2,1,0:T(8,128)(2,1)} %pairs.1), calls=%async_computation.1 | async-start | bytes 262144 | tf_op jit(solution)/shard_map/all_to_all | solution.py:485
  62.3 6.4 %slope.1.gs_hbm = bf16[512,1282]{1,0:T(8,128)(2,1)} custom-call(f32[512,1282]{1,0:T(8,128)} %get-tuple-element.23.pre_ref), custom_call_target="tpu_custom_call" | custom-call | flops 13127680 | bytes 5251072 | tf_op jit(solution)/shard_map/slope/pallas_call | solution.py:398
  68.7 5.3 %all-to-all-done.1.pair_ref = bf16[32,9,128]{2,1,0:T(8,128)(2,1)S(1)} async-done(((bf16[32,9,128]{2,1,0:T(8,128)(2,1)}), bf16[32,9,128]{2,1,0:T(8,128)(2,1)S(1)}, u32[]{:S(2)}, u32[]{:S(2)}) %all-to-all-start.1) | async-done | bytes 73760 | tf_op jit(solution)/shard_map/all_to_all | solution.py:485
  74.7 11.8 %backward.1 = (f32[72,512]{1,0:T(8,128)}, f32[6,4,128,128]{3,2,1,0:T(8,128)}, bf16[6,512,128]{2,1,0:T(8,128)(2,1)}, bf16[16,16,768]{2,1,0:T(8,128)(2,1)}) custom-call(s32[1]{0:T(128)} %bitcast.next_ref, bf16[32,9,128]{2,1,0:T(8,128)(2,1)} %get-tuple-element.20.pred_ref, bf16[72,512]{1,0:T(8,128)(2,1)} %bitcast.26, bf16[32,9,128]{2,1,0:T(8,128)(2,1)} %copy-done.2, ...), custom_call_target="tpu_custom_call" | custom-call | flops 88080384 | bytes 3145728 | tf_op jit(solution)/shard_map/backward/pallas_call | solution.py:418
  86.5 19.5 %all_to_all.26 = bf16[16,16,768]{2,1,0:T(8,128)(2,1)S(1)} all-to-all(bf16[16,16,768]{2,1,0:T(8,128)(2,1)} %get-tuple-element.24), channel_id=1, replica_groups=mesh['ens'=32,'lon'=16] {'lon'}, dimensions={0} | all-to-all | bytes 786432 | tf_op jit(solution)/shard_map/all_to_all | solution.py:485
  106.0 0.7 broadcast_in_dim.17
  106.8 8.2 %all-to-all-start.3 = ((bf16[32,4,768]{2,1,0:T(4,128)(2,1)}), bf16[32,4,768]{2,1,0:T(4,128)(2,1)S(1)}, u32[]{:S(2)}, u32[]{:S(2)}) async-start(bf16[32,4,768]{2,1,0:T(4,128)(2,1)} %broadcast_in_dim.17), calls=%async_computation.3 | async-start | bytes 393216 | tf_op jit(solution)/shard_map/all_to_all | solution.py:485
  115.6 8.2 %adjoint.1 = bf16[641,4,128]{2,1,0:T(4,128)(2,1)} custom-call(f32[6,4,128,128]{3,2,1,0:T(8,128)} %get-tuple-element.25.cot_hbm, bf16[16,768]{1,0:T(8,128)(2,1)} %get-tuple-element.31.hl_ref, bf16[16,768]{1,0:T(8,128)(2,1)} %get-tuple-element.30.hr_ref, f32[6,56,128]{2,1,0:T(8,128)} %bitcast_bitcast_fusion.wt_ref, ...), custom_call_target="tpu_custom_call" | custom-call | flops 88080384 | bytes 3145728 | tf_op jit(solution)/shard_map/adjoint/pallas_call | solution.py:438
  123.8 4.1 %all-to-all-done.3 = bf16[32,4,768]{2,1,0:T(4,128)(2,1)S(1)} async-done(((bf16[32,4,768]{2,1,0:T(4,128)(2,1)}), bf16[32,4,768]{2,1,0:T(4,128)(2,1)S(1)}, u32[]{:S(2)}, u32[]{:S(2)}) %all-to-all-start.3) | async-done | bytes 196640 | tf_op jit(solution)/shard_map/all_to_all | solution.py:485
  128.0 0.7 broadcast_in_dim.19
  128.7 4.3 %all-to-all-start.4 = ((bf16[16,4,768]{2,1,0:T(4,128)(2,1)}), bf16[16,4,768]{2,1,0:T(4,128)(2,1)S(1)}, u32[]{:S(2)}, u32[]{:S(2)}) async-start(bf16[16,4,768]{2,1,0:T(4,128)(2,1)} %broadcast_in_dim.19), calls=%async_computation.4 | async-start | bytes 196608 | tf_op jit(solution)/shard_map/all_to_all | solution.py:485
  133.1 0.7 reshape.25
  133.8 6.4 %all-to-all-done.4 = bf16[16,4,768]{2,1,0:T(4,128)(2,1)S(1)} async-done(((bf16[16,4,768]{2,1,0:T(4,128)(2,1)}), bf16[16,4,768]{2,1,0:T(4,128)(2,1)S(1)}, u32[]{:S(2)}, u32[]{:S(2)}) %all-to-all-start.4) | async-done | bytes 98336 | tf_op jit(solution)/shard_map/all_to_all | solution.py:485
  140.2 0.7 slice_bitcast_fusion
  (20 shorter events, 3.3 us)
Async XLA Ops:
  0.6 1.1 copy-start.1
  2.4 0.9 copy-start
  3.3 12.5 %collective-permute-start = (bf16[16,768]{1,0:T(8,128)(2,1)S(1)}, bf16[16,768]{1,0:T(8,128)(2,1)S(1)}, u32[]{:S(2)}, u32[]{:S(2)}) collective-permute-start(bf16[16,768]{1,0:T(8,128)(2,1)S(1)} %get-tuple-element.18), channel_id=1, source_target_pairs={{0,1},{1,2},{2,3},{3,4},{4,5},{5,6},{6,7},{7,8},{8,9},{9,10},{10,1... | collective-permute-start | bytes 73736 | tf_op jit(solution)/shard_map/ppermute | solution.py:453
  7.3 8.5 %collective-permute-start.1 = (bf16[16,768]{1,0:T(8,128)(2,1)S(1)}, bf16[16,768]{1,0:T(8,128)(2,1)S(1)}, u32[]{:S(2)}, u32[]{:S(2)}) collective-permute-start(bf16[16,768]{1,0:T(8,128)(2,1)S(1)} %get-tuple-element.19), channel_id=1, source_target_pairs={{1,0},{2,1},{3,2},{4,3},{5,4},{6,5},{7,6},{8,7},{9,8},{10,9},{11,1... | collective-permute-start | bytes 73736 | tf_op jit(solution)/shard_map/ppermute | solution.py:453
  15.8 0.6 copy-start.4
  15.8 0.6 copy-start.5
  16.4 45.3 %copy-start.6 = (bf16[72,4,128]{2,1,0:T(4,128)(2,1)S(1)}, bf16[72,4,128]{2,1,0:T(4,128)(2,1)}, u32[]{:S(2)}) copy-start(bf16[72,4,128]{2,1,0:T(4,128)(2,1)} %param.8) | copy-start | bytes 221188
  57.4 16.6 %all-to-all-start.1 = ((bf16[32,9,128]{2,1,0:T(8,128)(2,1)}), bf16[32,9,128]{2,1,0:T(8,128)(2,1)S(1)}, u32[]{:S(2)}, u32[]{:S(2)}) async-start(bf16[32,9,128]{2,1,0:T(8,128)(2,1)} %pairs.1), calls=%async_computation.1 | async-start | bytes 262144 | tf_op jit(solution)/shard_map/all_to_all | solution.py:485
  74.0 0.7 copy-start.2
  106.8 21.2 %all-to-all-start.3 = ((bf16[32,4,768]{2,1,0:T(4,128)(2,1)}), bf16[32,4,768]{2,1,0:T(4,128)(2,1)S(1)}, u32[]{:S(2)}, u32[]{:S(2)}) async-start(bf16[32,4,768]{2,1,0:T(4,128)(2,1)} %broadcast_in_dim.17), calls=%async_computation.3 | async-start | bytes 393216 | tf_op jit(solution)/shard_map/all_to_all | solution.py:485
  115.6 17.4 %copy-start.3 = (f32[72,512]{1,0:T(8,128)S(1)}, f32[72,512]{1,0:T(8,128)}, u32[]{:S(2)}) copy-start(f32[72,512]{1,0:T(8,128)} %get-tuple-element.28) | copy-start | bytes 442372
  128.7 11.5 %all-to-all-start.4 = ((bf16[16,4,768]{2,1,0:T(4,128)(2,1)}), bf16[16,4,768]{2,1,0:T(4,128)(2,1)S(1)}, u32[]{:S(2)}, u32[]{:S(2)}) async-start(bf16[16,4,768]{2,1,0:T(4,128)(2,1)} %broadcast_in_dim.19), calls=%async_computation.4 | async-start | bytes 196608 | tf_op jit(solution)/shard_map/all_to_all | solution.py:485

commit v2 on v1

--- a/solution.py
+++ b/solution.py
@@ -34,7 +34,10 @@
 
 
 def edges(blocks):
-    return jnp.concatenate([x[-3:] for x in blocks], 0), jnp.concatenate([x[:3] for x in blocks], 0)
+    fill = [jnp.zeros((16 - 3 * len(blocks), blocks[0].shape[1]), F32)]
+    last = jnp.concatenate([x[-3:] for x in blocks] + fill, 0)
+    first = jnp.concatenate([x[:3] for x in blocks] + fill, 0)
+    return last.astype(BF16), first.astype(BF16)
 
 
 def pack_kernel(f_ref, ft_ref, right_ref, left_ref, flat_ref):
@@ -52,10 +55,7 @@
             x = flat_ref[pl.ds(tile * tall + r, LANES, stride=nrows), :].astype(BF16)
             blocks.append(mm(eye, x, NT))
             ft_ref[r, :, cols(tile)] = blocks[r].astype(BF16)
-        fill = jnp.zeros((16 - 3 * nrows, LANES), F32)
-        last, first = edges(blocks)
-        right_ref[:, cols(tile)] = jnp.concatenate([last, fill], 0).astype(BF16)
-        left_ref[:, cols(tile)] = jnp.concatenate([first, fill], 0).astype(BF16)
+        right_ref[:, cols(tile)], left_ref[:, cols(tile)] = edges(blocks)
 
 
 def fill_edges(x_ref, left, right):
@@ -210,9 +210,9 @@
 
 
 def backward_kernel(
-    channels, members, next_ref, pred_ref, obs_ref, pair_ref, hl_ref, hr_ref, wt_ref,
+    channels, members, pred_ref, obs_ref, pair_ref, hl_ref, hr_ref, wt_ref,
     up_hbm, down_hbm, head_hbm, xhat_hbm, inv_hbm, gs_hbm, ft_hbm,
-    score_ref, cot_hbm, direct_hbm, out_ref,
+    score_ref, cot_hbm, direct_hbm, right_ref, left_ref, out_ref,
     dpre_ref, cot_ref, direct_ref, sums_ref, x_ref,
     up_ref, down_ref, head_ref, xhat_ref, inv_ref, gs_ref, ft_ref, sems,
 ):
@@ -272,11 +272,15 @@
     for tile in range(tiles):
         sums_ref[tile, 48:, :] = jnp.zeros((sums_ref.shape[1] - 48, LANES), F32)
         sums_ref[tile, 49:50, :] = gains[tile]
+        right_ref[:, cols(tile)], left_ref[:, cols(tile)] = edges([cot_ref[tile, r] for r in range(nrows)])
 
 
     fill_fields(x_ref, ft_ref, hl_ref, hr_ref)
     add_taps(x_ref, cot_ref, sums_ref)
-    send(next_ref[0], cot_ref, sums_ref, out_ref)
+    pieces, deep, _ = out_ref.shape
+    for tile in range(tiles):
+        for p in range(pieces):
+            out_ref[p, :, cols(tile)] = sums_ref[tile, p * deep : (p + 1) * deep, :].astype(BF16)
     wait_all(stores)
 
 
@@ -303,18 +307,6 @@
     lax.fori_loop(0, tiles, body, 0)
 
 
-def send(right, cot_ref, sums_ref, out_ref):
-    tiles, nrows, _, _ = cot_ref.shape
-    pieces, tall, _ = out_ref.shape
-    deep = tall - 3 * nrows
-    for tile in range(tiles):
-        last, first = edges([cot_ref[tile, r] for r in range(nrows)])
-        for p in range(pieces):
-            edge = jnp.where(right == p, last, first)
-            share = sums_ref[tile, p * deep : (p + 1) * deep, :]
-            out_ref[p, :, cols(tile)] = jnp.concatenate([edge, share], 0).astype(BF16)
-
-
 def adjoint_kernel(
     cot_hbm, hl_ref, hr_ref, wt_ref, direct_hbm, out_ref, x_ref, gather_ref, row_ref, direct_ref, sems
 ):
@@ -407,21 +399,21 @@
     )(pre)
 
 
-def backward(members, pieces, right, pred, obs, pair, hl, hr, wt, up, down, head, xhat, inv, gslope, ft):
+def backward(members, pieces, pred, obs, pair, hl, hr, wt, up, down, head, xhat, inv, gslope, ft):
     tiles, nrows, lons, _ = xhat.shape
     points, wide = nrows * lons, tiles * LANES
     channels, hiddens = down.shape
     sums = pieces * (4 if 4 * pieces >= 56 else 16)
-    tall = 3 * nrows + sums // pieces
+    edge = ((16, wide), BF16, VM)
     direct = ((tiles, points, LANES), BF16)
     far = (up, down, head, xhat, inv, gslope, ft)
     return call(
-        functools.partial(backward_kernel, channels, members), "backward", [pltpu.SMEM] + [VM] * 6 + [HB] * 7,
-        [(obs.shape, F32, VM), (xhat.shape, F32, HB), (*direct, HB), ((pieces, tall, wide), BF16, VM)],
+        functools.partial(backward_kernel, channels, members), "backward", [VM] * 6 + [HB] * 7,
+        [(obs.shape, F32, VM), (xhat.shape, F32, HB), (*direct, HB), edge, edge, ((pieces, sums // pieces, wide), BF16, VM)],
         [((points, hiddens), BF16), (xhat.shape, F32), direct, ((tiles, sums, LANES), F32), (padded_shape(ft), F32)]
         + [(v.shape, v.dtype) for v in far],
         9, 224 * xhat.size, 8 * xhat.size,
-    )(right, pred, obs, pair, hl, hr, wt, *far)
+    )(pred, obs, pair, hl, hr, wt, *far)
 
 
 def pairs(p):
@@ -467,16 +459,12 @@
     met = exchange(pred, "ens")
     pair = exchange(pairs(met), "ens")
     gslope = gelu_slope(pre)
-    here = lax.axis_index("lon")
-    before, after = (here + pieces - 1) % pieces, (here + 1) % pieces
-    score, cot, direct, sent = backward(
-        members, pieces, after[None], pred, observed.reshape(nvars, -1), pair, hl, hr, wt,
+    score, cot, direct, to_right, to_left, shares = backward(
+        members, pieces, pred, observed.reshape(nvars, -1), pair, hl, hr, wt,
         up_weight, down_weight, head_weight, xhat, inv, gslope, ft,
     )
-    met = exchange(sent, "lon")
     field_out, total = reduce_beside(
-        jnp.sum(met[:, 3 * nrows :].astype(F32), 0).astype(BF16),
-        lambda: adjoint(channels, cot, met[before], met[after], wt, direct),
+        shares, swap_edges(to_right, to_left), lambda cl, cr: adjoint(channels, cot, cl, cr, wt, direct)
     )
     return (field_out[None], score.reshape(1, nvars, nrows, lons), total[:49, :channels].T, total[49, :channels])
 
@@ -485,11 +473,12 @@
     return lax.all_to_all(x, axis, 0, 0, tiled=True)
 
 
-def reduce_beside(mine, work):
-    deep, wide = mine.shape
-    pieces = lax.axis_size("lon")
+def reduce_beside(shares, edges_in, work):
+    pieces, deep, wide = shares.shape
+    parts, edges_in = lax.optimization_barrier((exchange(shares, "lon"), edges_in))
+    mine = jnp.sum(parts.astype(F32), 0).astype(BF16)
     parts = exchange(jnp.broadcast_to(mine, (lax.axis_size("ens"), deep, wide)), "ens")
-    parts, done = lax.optimization_barrier((parts, work()))
+    parts, done = lax.optimization_barrier((parts, work(*edges_in)))
     mine = jnp.sum(parts.astype(F32), 0).astype(BF16)
     total = exchange(jnp.broadcast_to(mine, (pieces, deep, wide)), "lon").astype(F32)
     return done, total.reshape(pieces * deep, wide)

time: 142 us -> 143 us (level)
  blocking collectives: 48.6 us -> 29.2 us
  starting transfers between devices: 27 us -> 45.7 us
  waiting for transfers between devices: 15.8 us -> 17.7 us
    all_to_all x2 -> x1, blocking collectives: 48.6 us -> 29.2 us  [exchange(): return lax.all_to_all(x, axis, 0, 0, tiled=True)]
    all_to_all x3 -> x4, starting transfers between devices: 16.8 us -> 26.4 us  [exchange(): return lax.all_to_all(x, axis, 0, 0, tiled=True)]
    ppermute x1 -> x2, starting transfers between devices: 6.14 us -> 12.1 us  [swap_edges(): lax.ppermute(to_left, 'lon', down)]
    ppermute x1 -> x2, starting transfers between devices: 4.01 us -> 7.27 us  [swap_edges(): lax.ppermute(to_right, 'lon', up)]
    all_to_all x3 -> x4, waiting for transfers between devices: 15.8 us -> 16.6 us  [exchange(): return lax.all_to_all(x, axis, 0, 0, tiled=True)]
    unnamed x15 -> x19, local copies, waits for them, and re-layouts: 3.88 us -> 3.88 us
  transfers between devices with their start and end apart: 5 -> 8, of which waited for: 3 -> 4; matrix products, arithmetic and copies ran while one was open for 3% -> 3% of each run, Pallas kernels for 10% -> 10%
where the time goes in v2:
time: 143 us; the launch traced here: 142 us
  starting transfers between devices  45.7 us (32%)
  Pallas kernels  38.7 us (27%)
  blocking collectives  29.2 us (20%)
  waiting for transfers between devices  17.7 us (12%)
  local copies, waits for them, and re-layouts  7.98 us (6%)
  other arithmetic  1.77 us (1%)
    all_to_all x1, blocking collectives, exchange(): return lax.all_to_all(x, axis, 0, 0, tiled=True)  29.2 us
    all_to_all x4, starting transfers between devices, exchange(): return lax.all_to_all(x, axis, 0, 0, tiled=True)  26.4 us
    all_to_all x4, waiting for transfers between devices, exchange(): return lax.all_to_all(x, axis, 0, 0, tiled=True)  16.6 us
    ppermute x2, starting transfers between devices, swap_edges(): lax.ppermute(to_left, 'lon', down)  12.1 us
    pallas_call x1, Pallas kernels, backward(): call(functools.partial(backward_kernel, channels, members), 'backward', [...  11.7 us
    pallas_call x1, Pallas kernels, forward(): call(functools.partial(forward_kernel, channels), 'forward', [HB] + [VM]...  10.1 us
    pallas_call x1, Pallas kernels, adjoint(): call(adjoint_kernel, 'adjoint', [HB, VM, VM, VM, HB], [((channels, nrows,...  8.18 us
    ppermute x2, starting transfers between devices, swap_edges(): lax.ppermute(to_right, 'lon', up)  7.27 us
  transfers between devices with their start and end apart: 8, of which 4 were waited for; matrix products, arithmetic and copies ran while one was open for 3% of the time, Pallas kernels for 10%

profile of v2, /device:TPU:1, one launch (start us, length us, event | category | flops | bytes accessed | tf_op | source)
XLA Modules:
  0.0 141.9 jit_solution(11271677167540469352)
XLA Ops:
  0.6 1.1 copy-done.1
  2.4 0.9 copy-done
  3.3 4.0 %collective-permute-start = (bf16[16,768]{1,0:T(8,128)(2,1)S(1)}, bf16[16,768]{1,0:T(8,128)(2,1)S(1)}, u32[]{:S(2)}, u32[]{:S(2)}) collective-permute-start(bf16[16,768]{1,0:T(8,128)(2,1)S(1)} %get-tuple-element.23), channel_id=1, source_target_pairs={{0,1},{1,2},{2,3},{3,4},{4,5},{5,6},{6,7},{7,8},{8,9},{9,10},{10,1... | collective-permute-start | bytes 73736 | tf_op jit(solution)/shard_map/ppermute | solution.py:445
  7.3 6.1 %collective-permute-start.1 = (bf16[16,768]{1,0:T(8,128)(2,1)S(1)}, bf16[16,768]{1,0:T(8,128)(2,1)S(1)}, u32[]{:S(2)}, u32[]{:S(2)}) collective-permute-start(bf16[16,768]{1,0:T(8,128)(2,1)S(1)} %get-tuple-element.24), channel_id=1, source_target_pairs={{1,0},{2,1},{3,2},{4,3},{5,4},{6,5},{7,6},{8,7},{9,8},{10,9},{11,1... | collective-permute-start | bytes 73736 | tf_op jit(solution)/shard_map/ppermute | solution.py:445
  13.5 0.7 broadcast_in_dim.12
  14.2 1.6 %bitcast_bitcast_fusion.wt_ref = f32[6,56,128]{2,1,0:T(8,128)} fusion(f32[1,641]{1,0:T(1,128)S(1)} %broadcast_in_dim.12, f32[49,641]{1,0:T(8,128)} %bitcast.22), kind=kLoop, calls=%fused_computation | loop fusion | flops 344064 | bytes 300232 | tf_op jit(solution)/shard_map/transpose | solution.py:457
  16.4 10.1 %forward.1 = (bf16[32,9,128]{2,1,0:T(8,128)(2,1)}, f32[6,4,128,128]{3,2,1,0:T(8,128)}, f32[4,128,1]{2,1,0:T(8,128)}, f32[512,1282]{1,0:T(8,128)}) custom-call(bf16[4,128,768]{2,1,0:T(8,128)(2,1)} %copy-done, bf16[16,768]{1,0:T(8,128)(2,1)} %copy-done.4, bf16[16,768]{1,0:T(8,128)(2,1)} %copy-done.5, f32[6,56,128]{2,1,0:T(8,128)} %bitcast_bitcast_fusion.wt_ref, ...), custom_call_target="tpu_custom_call" | custom-call | tf_op jit(solution)/shard_map/forward/pallas_call | solution.py:379
  26.5 29.2 %all_to_all.25.p_ref = bf16[32,9,128]{2,1,0:T(8,128)(2,1)S(1)} all-to-all(bf16[32,9,128]{2,1,0:T(8,128)(2,1)} %get-tuple-element.25.pred_ref), channel_id=1, replica_groups=mesh['ens'=32,'lon'=16] {'ens'}, dimensions={0} | all-to-all | bytes 147456 | tf_op jit(solution)/shard_map/all_to_all | solution.py:473
  55.7 1.7 %pairs.1 = bf16[32,9,128]{2,1,0:T(8,128)(2,1)} custom-call(bf16[32,9,128]{2,1,0:T(8,128)(2,1)S(1)} %all_to_all.25.p_ref), custom_call_target="tpu_custom_call" | custom-call | tf_op jit(solution)/shard_map/pairs/pallas_call | solution.py:421
  57.4 4.3 %all-to-all-start.1 = ((bf16[32,9,128]{2,1,0:T(8,128)(2,1)}), bf16[32,9,128]{2,1,0:T(8,128)(2,1)S(1)}, u32[]{:S(2)}, u32[]{:S(2)}) async-start(bf16[32,9,128]{2,1,0:T(8,128)(2,1)} %pairs.1), calls=%async_computation.1 | async-start | bytes 262144 | tf_op jit(solution)/shard_map/all_to_all | solution.py:473
  62.3 6.4 %slope.1.gs_hbm = bf16[512,1282]{1,0:T(8,128)(2,1)} custom-call(f32[512,1282]{1,0:T(8,128)} %get-tuple-element.28.pre_ref), custom_call_target="tpu_custom_call" | custom-call | flops 13127680 | bytes 5251072 | tf_op jit(solution)/shard_map/slope/pallas_call | solution.py:390
  68.7 5.3 %all-to-all-done.1.pair_ref = bf16[32,9,128]{2,1,0:T(8,128)(2,1)S(1)} async-done(((bf16[32,9,128]{2,1,0:T(8,128)(2,1)}), bf16[32,9,128]{2,1,0:T(8,128)(2,1)S(1)}, u32[]{:S(2)}, u32[]{:S(2)}) %all-to-all-start.1) | async-done | bytes 73760 | tf_op jit(solution)/shard_map/all_to_all | solution.py:473
  74.7 11.7 %backward.1 = (f32[72,512]{1,0:T(8,128)}, f32[6,4,128,128]{3,2,1,0:T(8,128)}, bf16[6,512,128]{2,1,0:T(8,128)(2,1)}, bf16[16,768]{1,0:T(8,128)(2,1)}, bf16[16,768...) custom-call(bf16[32,9,128]{2,1,0:T(8,128)(2,1)} %get-tuple-element.25.pred_ref, bf16[72,512]{1,0:T(8,128)(2,1)} %bitcast.21, ...), custom_call_target="tpu_custom_call" | custom-call | flops 88080384 | bytes 3145728 | tf_op jit(solution)/shard_map/backward/pallas_call | solution.py:410
  86.4 6.5 %all-to-all-start.2 = ((bf16[16,4,768]{2,1,0:T(4,128)(2,1)}), bf16[16,4,768]{2,1,0:T(4,128)(2,1)S(1)}, u32[]{:S(2)}, u32[]{:S(2)}) async-start(bf16[16,4,768]{2,1,0:T(4,128)(2,1)} %get-tuple-element.29), calls=%async_computation.2 | async-start | bytes 196608 | tf_op jit(solution)/shard_map/all_to_all | solution.py:473
  92.9 3.3 %collective-permute-start.2 = (bf16[16,768]{1,0:T(8,128)(2,1)}, bf16[16,768]{1,0:T(8,128)(2,1)S(1)}, u32[]{:S(2)}, u32[]{:S(2)}) collective-permute-start(bf16[16,768]{1,0:T(8,128)(2,1)} %get-tuple-element.30), channel_id=1, source_target_pairs={{0,1},{1,2},{2,3},{3,4},{4,5},{5,6},{6,7},{7,8},{8,9},{9,10},{10,1... | collective-permute-start | bytes 73736 | tf_op jit(solution)/shard_map/ppermute | solution.py:445
  96.1 5.9 %collective-permute-start.3 = (bf16[16,768]{1,0:T(8,128)(2,1)}, bf16[16,768]{1,0:T(8,128)(2,1)S(1)}, u32[]{:S(2)}, u32[]{:S(2)}) collective-permute-start(bf16[16,768]{1,0:T(8,128)(2,1)} %get-tuple-element.31), channel_id=1, source_target_pairs={{1,0},{2,1},{3,2},{4,3},{5,4},{6,5},{7,6},{8,7},{9,8},{10,9},{11,1... | collective-permute-start | bytes 73736 | tf_op jit(solution)/shard_map/ppermute | solution.py:445
  102.1 1.1 collective-permute-done.3.hr_ref
  103.3 0.7 broadcast_in_dim.13
  104.0 8.3 %all-to-all-start.3 = ((bf16[32,4,768]{2,1,0:T(4,128)(2,1)}), bf16[32,4,768]{2,1,0:T(4,128)(2,1)S(1)}, u32[]{:S(2)}, u32[]{:S(2)}) async-start(bf16[32,4,768]{2,1,0:T(4,128)(2,1)} %broadcast_in_dim.13), calls=%async_computation.3 | async-start | bytes 393216 | tf_op jit(solution)/shard_map/all_to_all | solution.py:473
  112.3 8.2 %adjoint.1 = bf16[641,4,128]{2,1,0:T(4,128)(2,1)} custom-call(f32[6,4,128,128]{3,2,1,0:T(8,128)} %get-tuple-element.33.cot_hbm, bf16[16,768]{1,0:T(8,128)(2,1)} %copy-done.7, bf16[16,768]{1,0:T(8,128)(2,1)} %copy-done.8, f32[6,56,128]{2,1,0:T(8,128)} %bitcast_bitcast_fusion.wt_ref, bf16[6,512,128]{2,1,0:T(8,128)(2,1)} %get-tuple-element.36.direct_hbm), custom_call_target="tpu_custom_call" | custom-call | flops 88080384 | bytes 3145728 | tf_op jit(solution)/shard_map/adjoint/pallas_call | solution.py:430
  120.5 4.8 %all-to-all-done.3 = bf16[32,4,768]{2,1,0:T(4,128)(2,1)S(1)} async-done(((bf16[32,4,768]{2,1,0:T(4,128)(2,1)}), bf16[32,4,768]{2,1,0:T(4,128)(2,1)S(1)}, u32[]{:S(2)}, u32[]{:S(2)}) %all-to-all-start.3) | async-done | bytes 196640 | tf_op jit(solution)/shard_map/all_to_all | solution.py:473
  126.1 7.4 %all-to-all-start.4 = ((bf16[16,4,768]{2,1,0:T(4,128)(2,1)}), bf16[16,4,768]{2,1,0:T(4,128)(2,1)S(1)}, u32[]{:S(2)}, u32[]{:S(2)}) async-start(bf16[16,4,768]{2,1,0:T(4,128)(2,1)} %broadcast_in_dim.15), calls=%async_computation.4 | async-start | bytes 196608 | tf_op jit(solution)/shard_map/all_to_all | solution.py:473
  133.5 0.7 reshape.25
  134.2 6.4 %all-to-all-done.4 = bf16[16,4,768]{2,1,0:T(4,128)(2,1)S(1)} async-done(((bf16[16,4,768]{2,1,0:T(4,128)(2,1)}), bf16[16,4,768]{2,1,0:T(4,128)(2,1)S(1)}, u32[]{:S(2)}, u32[]{:S(2)}) %all-to-all-start.4) | async-done | bytes 98336 | tf_op jit(solution)/shard_map/all_to_all | solution.py:473
  (28 shorter events, 4.7 us)
Async XLA Ops:
  0.6 1.1 copy-start.1
  2.4 0.9 copy-start
  3.3 12.5 %collective-permute-start = (bf16[16,768]{1,0:T(8,128)(2,1)S(1)}, bf16[16,768]{1,0:T(8,128)(2,1)S(1)}, u32[]{:S(2)}, u32[]{:S(2)}) collective-permute-start(bf16[16,768]{1,0:T(8,128)(2,1)S(1)} %get-tuple-element.23), channel_id=1, source_target_pairs={{0,1},{1,2},{2,3},{3,4},{4,5},{5,6},{6,7},{7,8},{8,9},{9,10},{10,1... | collective-permute-start | bytes 73736 | tf_op jit(solution)/shard_map/ppermute | solution.py:445
  7.3 8.5 %collective-permute-start.1 = (bf16[16,768]{1,0:T(8,128)(2,1)S(1)}, bf16[16,768]{1,0:T(8,128)(2,1)S(1)}, u32[]{:S(2)}, u32[]{:S(2)}) collective-permute-start(bf16[16,768]{1,0:T(8,128)(2,1)S(1)} %get-tuple-element.24), channel_id=1, source_target_pairs={{1,0},{2,1},{3,2},{4,3},{5,4},{6,5},{7,6},{8,7},{9,8},{10,9},{11,1... | collective-permute-start | bytes 73736 | tf_op jit(solution)/shard_map/ppermute | solution.py:445
  15.8 0.6 copy-start.4
  15.8 0.6 copy-start.5
  16.4 45.3 %copy-start.6 = (bf16[72,4,128]{2,1,0:T(4,128)(2,1)S(1)}, bf16[72,4,128]{2,1,0:T(4,128)(2,1)}, u32[]{:S(2)}) copy-start(bf16[72,4,128]{2,1,0:T(4,128)(2,1)} %param.8) | copy-start | bytes 221188
  57.4 16.6 %all-to-all-start.1 = ((bf16[32,9,128]{2,1,0:T(8,128)(2,1)}), bf16[32,9,128]{2,1,0:T(8,128)(2,1)S(1)}, u32[]{:S(2)}, u32[]{:S(2)}) async-start(bf16[32,9,128]{2,1,0:T(8,128)(2,1)} %pairs.1), calls=%async_computation.1 | async-start | bytes 262144 | tf_op jit(solution)/shard_map/all_to_all | solution.py:473
  74.0 0.6 copy-start.2
  86.4 16.9 %all-to-all-start.2 = ((bf16[16,4,768]{2,1,0:T(4,128)(2,1)}), bf16[16,4,768]{2,1,0:T(4,128)(2,1)S(1)}, u32[]{:S(2)}, u32[]{:S(2)}) async-start(bf16[16,4,768]{2,1,0:T(4,128)(2,1)} %get-tuple-element.29), calls=%async_computation.2 | async-start | bytes 196608 | tf_op jit(solution)/shard_map/all_to_all | solution.py:473
  92.9 9.2 %collective-permute-start.2 = (bf16[16,768]{1,0:T(8,128)(2,1)}, bf16[16,768]{1,0:T(8,128)(2,1)S(1)}, u32[]{:S(2)}, u32[]{:S(2)}) collective-permute-start(bf16[16,768]{1,0:T(8,128)(2,1)} %get-tuple-element.30), channel_id=1, source_target_pairs={{0,1},{1,2},{2,3},{3,4},{4,5},{5,6},{6,7},{7,8},{8,9},{9,10},{10,1... | collective-permute-start | bytes 73736 | tf_op jit(solution)/shard_map/ppermute | solution.py:445
  96.1 7.1 %collective-permute-start.3 = (bf16[16,768]{1,0:T(8,128)(2,1)}, bf16[16,768]{1,0:T(8,128)(2,1)S(1)}, u32[]{:S(2)}, u32[]{:S(2)}) collective-permute-start(bf16[16,768]{1,0:T(8,128)(2,1)} %get-tuple-element.31), channel_id=1, source_target_pairs={{1,0},{2,1},{3,2},{4,3},{5,4},{6,5},{7,6},{8,7},{9,8},{10,9},{11,1... | collective-permute-start | bytes 73736 | tf_op jit(solution)/shard_map/ppermute | solution.py:445
  102.1 10.2 %copy-start.7 = (bf16[16,768]{1,0:T(8,128)(2,1)}, bf16[16,768]{1,0:T(8,128)(2,1)S(1)}, u32[]{:S(2)}) copy-start(bf16[16,768]{1,0:T(8,128)(2,1)S(1)} %collective-permute-done.2.hl_ref) | copy-start | bytes 73732
  103.2 9.1 %copy-start.8 = (bf16[16,768]{1,0:T(8,128)(2,1)}, bf16[16,768]{1,0:T(8,128)(2,1)S(1)}, u32[]{:S(2)}) copy-start(bf16[16,768]{1,0:T(8,128)(2,1)S(1)} %collective-permute-done.3.hr_ref) | copy-start | bytes 73732
  104.0 21.3 %all-to-all-start.3 = ((bf16[32,4,768]{2,1,0:T(4,128)(2,1)}), bf16[32,4,768]{2,1,0:T(4,128)(2,1)S(1)}, u32[]{:S(2)}, u32[]{:S(2)}) async-start(bf16[32,4,768]{2,1,0:T(4,128)(2,1)} %broadcast_in_dim.13), calls=%async_computation.3 | async-start | bytes 393216 | tf_op jit(solution)/shard_map/all_to_all | solution.py:473
  112.3 21.2 %copy-start.3 = (f32[72,512]{1,0:T(8,128)S(1)}, f32[72,512]{1,0:T(8,128)}, u32[]{:S(2)}) copy-start(f32[72,512]{1,0:T(8,128)} %get-tuple-element.38) | copy-start | bytes 442372
  126.1 14.5 %all-to-all-start.4 = ((bf16[16,4,768]{2,1,0:T(4,128)(2,1)}), bf16[16,4,768]{2,1,0:T(4,128)(2,1)S(1)}, u32[]{:S(2)}, u32[]{:S(2)}) async-start(bf16[16,4,768]{2,1,0:T(4,128)(2,1)} %broadcast_in_dim.15), calls=%async_computation.4 | async-start | bytes 196608 | tf_op jit(solution)/shard_map/all_to_all | solution.py:473

commit v3 on v1

--- a/solution.py
+++ b/solution.py
@@ -105,11 +105,11 @@
 
 
 def forward_kernel(
-    channels, ft_hbm, hl_ref, hr_ref, wt_ref, up_hbm, down_hbm, head_hbm,
+    channels, ft_hbm, hl_hbm, hr_hbm, wt_hbm, up_hbm, down_hbm, head_hbm,
     pred_ref, xhat_hbm, inv_hbm, pre_hbm,
-    x_ref, normed_ref, hidden_ref, xhat_ref, inv_ref, pre_ref, up_ref, down_ref, head_ref, ft_ref, sems,
+    x_ref, normed_ref, hidden_ref, xhat_ref, inv_ref, pre_ref, up_ref, down_ref, head_ref, ft_ref, hl_ref, hr_ref, wt_ref, sems,
 ):
-    fields = start_all([(ft_hbm, ft_ref)], sems, 6)
+    fields = start_all([(hl_hbm, hl_ref), (hr_hbm, hr_ref), (ft_hbm, ft_ref), (wt_hbm, wt_ref)], sems, 6)
     loads = start_all([(up_hbm, up_ref), (down_hbm, down_ref), (head_hbm, head_ref)], sems, 0)
     nrows, lons, wide = ft_ref.shape
     tiles = wide // LANES
@@ -210,16 +210,20 @@
 
 
 def backward_kernel(
-    channels, members, next_ref, pred_ref, obs_ref, pair_ref, hl_ref, hr_ref, wt_ref,
+    channels, members, next_ref, pred_hbm, obs_hbm, pair_hbm, hl_hbm, hr_hbm, wt_hbm,
     up_hbm, down_hbm, head_hbm, xhat_hbm, inv_hbm, gs_hbm, ft_hbm,
     score_ref, cot_hbm, direct_hbm, out_ref,
     dpre_ref, cot_ref, direct_ref, sums_ref, x_ref,
+    pred_ref, obs_ref, pair_ref, hl_ref, hr_ref, wt_ref,
     up_ref, down_ref, head_ref, xhat_ref, inv_ref, gs_ref, ft_ref, sems,
 ):
+    small = start_all([(pred_hbm, pred_ref), (obs_hbm, obs_ref), (pair_hbm, pair_ref)], sems, 9)
     first = start_all([(head_hbm, head_ref), (down_hbm, down_ref)], sems, 2)
     second = start_all([(gs_hbm, gs_ref)], sems, 4)
     third = start_all([(up_hbm, up_ref)], sems, 5)
     fourth = start_all([(xhat_hbm, xhat_ref), (inv_hbm, inv_ref), (ft_hbm, ft_ref)], sems, 6)
+    fourth += start_all([(hl_hbm, hl_ref), (hr_hbm, hr_ref), (wt_hbm, wt_ref)], sems, 12)
+    wait_all(small)
     tiles, nrows, lons, _ = xhat_ref.shape
     points = nrows * lons
     pieces, deep, _ = pred_ref.shape
@@ -385,10 +389,11 @@
     channels, hiddens = down.shape
     xhat, inv, pre = ((wide // LANES, nrows, lons, LANES), F32), ((nrows, lons, 1), F32), ((points, hiddens), F32)
     return call(
-        functools.partial(forward_kernel, channels), "forward", [HB] + [VM] * 3 + [HB] * 3,
+        functools.partial(forward_kernel, channels), "forward", [HB] * 7,
         [((members, head.shape[0] * nrows // members, lons), BF16, VM), (*xhat, HB), (*inv, HB), (*pre, HB)],
         [(padded_shape(ft), F32), ((points, wide), BF16), ((points, hiddens), BF16), xhat, inv, pre,
-         (up.shape, BF16), (down.shape, BF16), (head.shape, BF16), (ft.shape, BF16)], 7,
+         (up.shape, BF16), (down.shape, BF16), (head.shape, BF16)]
+        + [(v.shape, v.dtype) for v in (ft, hl, hr, wt)], 10,
     )(ft, hl, hr, wt, up, down, head)
 
 
@@ -414,14 +419,14 @@
     sums = pieces * (4 if 4 * pieces >= 56 else 16)
     tall = 3 * nrows + sums // pieces
     direct = ((tiles, points, LANES), BF16)
-    far = (up, down, head, xhat, inv, gslope, ft)
+    far = (pred, obs, pair, hl, hr, wt, up, down, head, xhat, inv, gslope, ft)
     return call(
-        functools.partial(backward_kernel, channels, members), "backward", [pltpu.SMEM] + [VM] * 6 + [HB] * 7,
+        functools.partial(backward_kernel, channels, members), "backward", [pltpu.SMEM] + [HB] * 13,
         [(obs.shape, F32, VM), (xhat.shape, F32, HB), (*direct, HB), ((pieces, tall, wide), BF16, VM)],
         [((points, hiddens), BF16), (xhat.shape, F32), direct, ((tiles, sums, LANES), F32), (padded_shape(ft), F32)]
         + [(v.shape, v.dtype) for v in far],
-        9, 224 * xhat.size, 8 * xhat.size,
-    )(right, pred, obs, pair, hl, hr, wt, *far)
+        15, 224 * xhat.size, 8 * xhat.size,
+    )(right, *far)
 
 
 def pairs(p):

time: 142 us -> 141 us (level)
  Pallas kernels: 38.9 us -> 37.1 us
where the time goes in v3:
time: 141 us; the launch traced here: 140 us
  blocking collectives  48.6 us (34%)
  Pallas kernels  37.1 us (26%)
  starting transfers between devices  27 us (19%)
  waiting for transfers between devices  15.8 us (11%)
  local copies, waits for them, and re-layouts  8.62 us (6%)
  other arithmetic  1.79 us (1%)
    all_to_all x2, blocking collectives, exchange(): return lax.all_to_all(x, axis, 0, 0, tiled=True)  48.6 us
    all_to_all x3, starting transfers between devices, exchange(): return lax.all_to_all(x, axis, 0, 0, tiled=True)  16.8 us
    all_to_all x3, waiting for transfers between devices, exchange(): return lax.all_to_all(x, axis, 0, 0, tiled=True)  15.8 us
    pallas_call x1, Pallas kernels, backward(): call(functools.partial(backward_kernel, channels, members), 'backward', [...  10.9 us
    pallas_call x1, Pallas kernels, forward(): call(functools.partial(forward_kernel, channels), 'forward', [HB] * 7, [(...  9.22 us
    pallas_call x1, Pallas kernels, adjoint(): call(adjoint_kernel, 'adjoint', [HB, VM, VM, VM, HB], [((channels, nrows,...  8.18 us
    pallas_call x1, Pallas kernels, gelu_slope(): pl.pallas_call(slope_kernel, name='slope', grid=(8,), out_shape=jax.Shape...  6.4 us
    ppermute x1, starting transfers between devices, swap_edges(): lax.ppermute(to_left, 'lon', down)  6.14 us
  transfers between devices with their start and end apart: 5, of which 3 were waited for; matrix products, arithmetic and copies ran while one was open for 3% of the time, Pallas kernels for 10%

profile of v3, /device:TPU:1, one launch (start us, length us, event | category | flops | bytes accessed | tf_op | source)
XLA Modules:
  0.0 139.8 jit_solution(137205131711785775)
XLA Ops:
  0.6 1.1 copy-done.1
  1.7 0.7 pack.1
  2.4 0.9 copy-done
  3.3 4.0 %collective-permute-start = (bf16[16,768]{1,0:T(8,128)(2,1)S(1)}, bf16[16,768]{1,0:T(8,128)(2,1)S(1)}, u32[]{:S(2)}, u32[]{:S(2)}) collective-permute-start(bf16[16,768]{1,0:T(8,128)(2,1)S(1)} %get-tuple-element.18), channel_id=1, source_target_pairs={{0,1},{1,2},{2,3},{3,4},{4,5},{5,6},{6,7},{7,8},{8,9},{9,10},{10,1... | collective-permute-start | bytes 73736 | tf_op jit(solution)/shard_map/ppermute | solution.py:458
  7.3 6.1 %collective-permute-start.1 = (bf16[16,768]{1,0:T(8,128)(2,1)S(1)}, bf16[16,768]{1,0:T(8,128)(2,1)S(1)}, u32[]{:S(2)}, u32[]{:S(2)}) collective-permute-start(bf16[16,768]{1,0:T(8,128)(2,1)S(1)} %get-tuple-element.19), channel_id=1, source_target_pairs={{1,0},{2,1},{3,2},{4,3},{5,4},{6,5},{7,6},{8,7},{9,8},{10,9},{11,1... | collective-permute-start | bytes 73736 | tf_op jit(solution)/shard_map/ppermute | solution.py:458
  13.5 0.7 broadcast_in_dim.16
  14.2 1.6 %bitcast_bitcast_fusion.wt_hbm.wt_ref = f32[6,56,128]{2,1,0:T(8,128)} fusion(f32[1,641]{1,0:T(1,128)S(1)} %broadcast_in_dim.16, f32[49,641]{1,0:T(8,128)} %bitcast.27), kind=kLoop, calls=%fused_computation | loop fusion | flops 344064 | bytes 300232 | tf_op jit(solution)/shard_map/transpose | solution.py:470
  16.4 9.2 %forward.1 = (bf16[32,9,128]{2,1,0:T(8,128)(2,1)}, f32[6,4,128,128]{3,2,1,0:T(8,128)}, f32[4,128,1]{2,1,0:T(8,128)}, f32[512,1282]{1,0:T(8,128)}) custom-call(bf16[4,128,768]{2,1,0:T(8,128)(2,1)} %copy-done, bf16[16,768]{1,0:T(8,128)(2,1)} %copy-done.4, bf16[16,768]{1,0:T(8,128)(2,1)} %copy-done.5, f32[6,56,128]{2,1,0:T(8,128)} %bitcast_bitcast_fusion.wt_hbm.wt_ref, ...), custom_call_target="tpu_custom_call" | custom-call | tf_op jit(solution)/shard_map/forward/pallas_call | solution.py:391
  25.6 29.2 %all_to_all.25.p_ref = bf16[32,9,128]{2,1,0:T(8,128)(2,1)S(1)} all-to-all(bf16[32,9,128]{2,1,0:T(8,128)(2,1)} %get-tuple-element.20.pred_hbm), channel_id=1, replica_groups=mesh['ens'=32,'lon'=16] {'ens'}, dimensions={0} | all-to-all | bytes 147456 | tf_op jit(solution)/shard_map/all_to_all | solution.py:490
  54.8 1.7 %pairs.1 = bf16[32,9,128]{2,1,0:T(8,128)(2,1)} custom-call(bf16[32,9,128]{2,1,0:T(8,128)(2,1)S(1)} %all_to_all.25.p_ref), custom_call_target="tpu_custom_call" | custom-call | tf_op jit(solution)/shard_map/pairs/pallas_call | solution.py:434
  56.5 4.3 %all-to-all-start.1 = ((bf16[32,9,128]{2,1,0:T(8,128)(2,1)}), bf16[32,9,128]{2,1,0:T(8,128)(2,1)S(1)}, u32[]{:S(2)}, u32[]{:S(2)}) async-start(bf16[32,9,128]{2,1,0:T(8,128)(2,1)} %pairs.1), calls=%async_computation.1 | async-start | bytes 262144 | tf_op jit(solution)/shard_map/all_to_all | solution.py:490
  61.4 6.4 %slope.1.gs_hbm = bf16[512,1282]{1,0:T(8,128)(2,1)} custom-call(f32[512,1282]{1,0:T(8,128)} %get-tuple-element.23.pre_ref), custom_call_target="tpu_custom_call" | custom-call | flops 13127680 | bytes 5251072 | tf_op jit(solution)/shard_map/slope/pallas_call | solution.py:403
  67.9 5.3 %all-to-all-done.1.pair_hbm = bf16[32,9,128]{2,1,0:T(8,128)(2,1)S(1)} async-done(((bf16[32,9,128]{2,1,0:T(8,128)(2,1)}), bf16[32,9,128]{2,1,0:T(8,128)(2,1)S(1)}, u32[]{:S(2)}, u32[]{:S(2)}) %all-to-all-start.1) | async-done | bytes 73760 | tf_op jit(solution)/shard_map/all_to_all | solution.py:490
  73.8 10.9 %backward.1 = (f32[72,512]{1,0:T(8,128)}, f32[6,4,128,128]{3,2,1,0:T(8,128)}, bf16[6,512,128]{2,1,0:T(8,128)(2,1)}, bf16[16,16,768]{2,1,0:T(8,128)(2,1)}) custom-call(s32[1]{0:T(128)} %bitcast.next_ref, bf16[32,9,128]{2,1,0:T(8,128)(2,1)} %get-tuple-element.20.pred_hbm, bf16[72,512]{1,0:T(8,128)(2,1)} %bitcast.26, bf16[32,9,128]{2,1,0:T(8,128)(2,1)} %copy-done.2, ...), custom_call_target="tpu_custom_call" | custom-call | flops 88080384 | bytes 3145728 | tf_op jit(solution)/shard_map/backward/pallas_call | solution.py:423
  84.7 19.5 %all_to_all.26 = bf16[16,16,768]{2,1,0:T(8,128)(2,1)S(1)} all-to-all(bf16[16,16,768]{2,1,0:T(8,128)(2,1)} %get-tuple-element.24), channel_id=1, replica_groups=mesh['ens'=32,'lon'=16] {'lon'}, dimensions={0} | all-to-all | bytes 786432 | tf_op jit(solution)/shard_map/all_to_all | solution.py:490
  104.3 0.7 broadcast_in_dim.17
  105.0 8.2 %all-to-all-start.3 = ((bf16[32,4,768]{2,1,0:T(4,128)(2,1)}), bf16[32,4,768]{2,1,0:T(4,128)(2,1)S(1)}, u32[]{:S(2)}, u32[]{:S(2)}) async-start(bf16[32,4,768]{2,1,0:T(4,128)(2,1)} %broadcast_in_dim.17), calls=%async_computation.3 | async-start | bytes 393216 | tf_op jit(solution)/shard_map/all_to_all | solution.py:490
  113.9 8.2 %adjoint.1 = bf16[641,4,128]{2,1,0:T(4,128)(2,1)} custom-call(f32[6,4,128,128]{3,2,1,0:T(8,128)} %get-tuple-element.25.cot_hbm, bf16[16,768]{1,0:T(8,128)(2,1)} %get-tuple-element.31.hl_ref, bf16[16,768]{1,0:T(8,128)(2,1)} %get-tuple-element.30.hr_ref, f32[6,56,128]{2,1,0:T(8,128)} %bitcast_bitcast_fusion.wt_hbm.wt_ref, ...), custom_call_target="tpu_custom_call" | custom-call | flops 88080384 | bytes 3145728 | tf_op jit(solution)/shard_map/adjoint/pallas_call | solution.py:443
  122.1 4.1 %all-to-all-done.3 = bf16[32,4,768]{2,1,0:T(4,128)(2,1)S(1)} async-done(((bf16[32,4,768]{2,1,0:T(4,128)(2,1)}), bf16[32,4,768]{2,1,0:T(4,128)(2,1)S(1)}, u32[]{:S(2)}, u32[]{:S(2)}) %all-to-all-start.3) | async-done | bytes 196640 | tf_op jit(solution)/shard_map/all_to_all | solution.py:490
  126.3 0.7 broadcast_in_dim.19
  127.0 4.3 %all-to-all-start.4 = ((bf16[16,4,768]{2,1,0:T(4,128)(2,1)}), bf16[16,4,768]{2,1,0:T(4,128)(2,1)S(1)}, u32[]{:S(2)}, u32[]{:S(2)}) async-start(bf16[16,4,768]{2,1,0:T(4,128)(2,1)} %broadcast_in_dim.19), calls=%async_computation.4 | async-start | bytes 196608 | tf_op jit(solution)/shard_map/all_to_all | solution.py:490
  131.3 0.7 reshape.25
  132.1 6.4 %all-to-all-done.4 = bf16[16,4,768]{2,1,0:T(4,128)(2,1)S(1)} async-done(((bf16[16,4,768]{2,1,0:T(4,128)(2,1)}), bf16[16,4,768]{2,1,0:T(4,128)(2,1)S(1)}, u32[]{:S(2)}, u32[]{:S(2)}) %all-to-all-start.4) | async-done | bytes 98336 | tf_op jit(solution)/shard_map/all_to_all | solution.py:490
  138.5 0.7 slice_bitcast_fusion
  (20 shorter events, 3.3 us)
Async XLA Ops:
  0.6 1.1 copy-start.1
  2.4 0.9 copy-start
  3.3 12.5 %collective-permute-start = (bf16[16,768]{1,0:T(8,128)(2,1)S(1)}, bf16[16,768]{1,0:T(8,128)(2,1)S(1)}, u32[]{:S(2)}, u32[]{:S(2)}) collective-permute-start(bf16[16,768]{1,0:T(8,128)(2,1)S(1)} %get-tuple-element.18), channel_id=1, source_target_pairs={{0,1},{1,2},{2,3},{3,4},{4,5},{5,6},{6,7},{7,8},{8,9},{9,10},{10,1... | collective-permute-start | bytes 73736 | tf_op jit(solution)/shard_map/ppermute | solution.py:458
  7.3 8.5 %collective-permute-start.1 = (bf16[16,768]{1,0:T(8,128)(2,1)S(1)}, bf16[16,768]{1,0:T(8,128)(2,1)S(1)}, u32[]{:S(2)}, u32[]{:S(2)}) collective-permute-start(bf16[16,768]{1,0:T(8,128)(2,1)S(1)} %get-tuple-element.19), channel_id=1, source_target_pairs={{1,0},{2,1},{3,2},{4,3},{5,4},{6,5},{7,6},{8,7},{9,8},{10,9},{11,1... | collective-permute-start | bytes 73736 | tf_op jit(solution)/shard_map/ppermute | solution.py:458
  15.8 0.6 copy-start.4
  15.8 0.6 copy-start.5
  16.4 44.4 %copy-start.6 = (bf16[72,4,128]{2,1,0:T(4,128)(2,1)S(1)}, bf16[72,4,128]{2,1,0:T(4,128)(2,1)}, u32[]{:S(2)}) copy-start(bf16[72,4,128]{2,1,0:T(4,128)(2,1)} %param.8) | copy-start | bytes 221188
  56.5 16.6 %all-to-all-start.1 = ((bf16[32,9,128]{2,1,0:T(8,128)(2,1)}), bf16[32,9,128]{2,1,0:T(8,128)(2,1)S(1)}, u32[]{:S(2)}, u32[]{:S(2)}) async-start(bf16[32,9,128]{2,1,0:T(8,128)(2,1)} %pairs.1), calls=%async_computation.1 | async-start | bytes 262144 | tf_op jit(solution)/shard_map/all_to_all | solution.py:490
  73.1 0.7 copy-start.2
  105.0 21.2 %all-to-all-start.3 = ((bf16[32,4,768]{2,1,0:T(4,128)(2,1)}), bf16[32,4,768]{2,1,0:T(4,128)(2,1)S(1)}, u32[]{:S(2)}, u32[]{:S(2)}) async-start(bf16[32,4,768]{2,1,0:T(4,128)(2,1)} %broadcast_in_dim.17), calls=%async_computation.3 | async-start | bytes 393216 | tf_op jit(solution)/shard_map/all_to_all | solution.py:490
  113.9 17.4 %copy-start.3 = (f32[72,512]{1,0:T(8,128)S(1)}, f32[72,512]{1,0:T(8,128)}, u32[]{:S(2)}) copy-start(f32[72,512]{1,0:T(8,128)} %get-tuple-element.28) | copy-start | bytes 442372
  127.0 11.5 %all-to-all-start.4 = ((bf16[16,4,768]{2,1,0:T(4,128)(2,1)}), bf16[16,4,768]{2,1,0:T(4,128)(2,1)S(1)}, u32[]{:S(2)}, u32[]{:S(2)}) async-start(bf16[16,4,768]{2,1,0:T(4,128)(2,1)} %broadcast_in_dim.19), calls=%async_computation.4 | async-start | bytes 196608 | tf_op jit(solution)/shard_map/all_to_all | solution.py:490
